TPU v7x, 256 devices: a whole 4x4x8 slice. The times are simulated.
256 devices in a mesh: spec: 16 (over x, z_lo, core), neuron: 16 (over z_hi, y).
Axes of the slice: x: 4, y: 4, z: 8 (z_hi: 4, z_lo: 2; z = z_hi * 2 + z_lo), core: 2. Of those that a mesh axis runs over, the one named last changes fastest.
Arguments:
- center: float32 [128, 8192], P('spec', 'neuron'), may hold values from -6 to 6
- radius: float32 [128, 8192], P('spec', 'neuron'), may hold values from 0.002 to 0.02
- weight: float32 [4096, 8192], P('neuron'), may hold values from -0.0625 to 0.0625
- bias: float32 [4096], P('neuron'), may hold values from -3 to 3
- out_weight: float32 [1000, 4096], P(None, 'neuron'), may hold values from -0.09375 to 0.09375
- masks: int32 [128, 4096], P(None, 'neuron'), may hold values from 0 to 2
- image_labels: int32 [128], replicated, may hold values from 0 to 999
- runner_up: int32 [8192], P('spec'), may hold values from 0 to 999
- spec_image: int32 [8192], P('spec'), may hold values from 0 to 127
Outputs:
- input_coeffs: float32 [8192, 8192], P('spec', 'neuron')
- margin_bounds: float32 [8192], P('spec')
All inputs are finite; a program needn't handle non-finite values.
Results may differ from a plain program's by a relative error of at most 0.000098.
Values sent between devices are 32-bit elements; how exact they have to be, the bound alone decides.
A program may use at most 128 MiB of HBM per device.

v0:
```python
import jax
import jax.numpy as jnp
from jax import lax
from jax.sharding import PartitionSpec as P


def relax(pre_center, pre_radius, masks):
    upper = pre_center + pre_radius
    lower = pre_center - pre_radius
    slope = jnp.clip(upper / (upper - lower), 0.0, 1.0)
    slopes = jnp.where(
        masks == 1, jnp.ones_like(slope), jnp.where(masks == 2, slope, jnp.zeros_like(slope))
    )
    offsets = jnp.where(masks == 2, slope * lower, jnp.zeros_like(slope))
    return (slopes, offsets)


def interval(center_full, radius_full, weight, bias, masks):
    highest = lax.Precision.HIGHEST
    dims = (((1,), (1,)), ((), ()))
    pre_center = lax.dot_general(center_full, weight, dims, precision=highest) + bias
    pre_radius = lax.dot_general(radius_full, jnp.abs(weight), dims, precision=highest)
    return relax(pre_center, pre_radius, masks)


def local(center, radius, weight, bias, out_weight, masks, image_labels, runner_up, spec_image):
    highest = lax.Precision.HIGHEST
    center_all, radius_all = (
        lax.all_gather(center, "spec", axis=0, tiled=True),
        lax.all_gather(radius, "spec", axis=0, tiled=True),
    )
    center_full, radius_full = (
        lax.all_gather(center_all, "neuron", axis=1, tiled=True),
        lax.all_gather(radius_all, "neuron", axis=1, tiled=True),
    )
    slopes_all, offsets_all = interval(center_full, radius_full, weight, bias, masks)
    true_class = jnp.take(image_labels, spec_image, axis=0)
    spec_coeff = jnp.take(out_weight, true_class, axis=0) - jnp.take(out_weight, runner_up, axis=0)
    scaled = spec_coeff * jnp.take(slopes_all, spec_image, axis=0)
    offset_rows = jnp.take(offsets_all, spec_image, axis=0)
    relax_part = -jnp.sum(jnp.minimum(spec_coeff, 0.0) * offset_rows, axis=1) + jnp.sum(
        scaled * bias, axis=1
    )
    input_coeffs = lax.psum_scatter(
        lax.dot_general(weight, scaled, (((0,), (1,)), ((), ())), precision=highest),
        "neuron",
        scatter_dimension=0,
        tiled=True,
    ).T
    center_rows = jnp.take(center_all, spec_image, axis=0)
    radius_rows = jnp.take(radius_all, spec_image, axis=0)
    input_part = jnp.sum(input_coeffs * center_rows - jnp.abs(input_coeffs) * radius_rows, axis=1)
    margin_bounds = lax.psum(input_part + relax_part, "neuron")
    return (input_coeffs, margin_bounds)


def solution(mesh):
    return jax.shard_map(
        local,
        mesh=mesh,
        in_specs=(
            P("spec", "neuron"),
            P("spec", "neuron"),
            P("neuron", None),
            P("neuron"),
            P(None, "neuron"),
            P(None, "neuron"),
            P(),
            P("spec"),
            P("spec"),
        ),
        out_specs=(P("spec", "neuron"), P("spec")),
        check_vma=False,
    )
```

profile of v0, /device:TPU:1, one launch (start us, length us, event | category | flops | bytes accessed | tf_op | source)
XLA Modules:
  0.0 473.5 jit_solution(12256146682107178975)
XLA Ops:
  7.2 24.2 %all_gather.14 = f32[128,512]{1,0:T(8,128)} all-gather(f32[8,512]{1,0:T(8,128)} %param.16), channel_id=1, replica_groups=mesh['spec'=16,'neuron'=16] {'spec'}, dimensions={0}, use_global_device_ids=true | all-gather | bytes 278528 | tf_op jit(solution)/shard_map/all_gather | solution.py:30
  31.4 0.0 all-gather.3.cloned.1.call-start
  31.5 18.9 %all_gather.12 = f32[128,512]{1,0:T(8,128)} all-gather(f32[8,512]{1,0:T(8,128)} %param.15), channel_id=1, replica_groups=mesh['spec'=16,'neuron'=16] {'spec'}, dimensions={0}, use_global_device_ids=true | all-gather | bytes 278528 | tf_op jit(solution)/shard_map/all_gather | solution.py:29
  50.5 0.0 reduce-scatter.2.cloned.1.call-start
  50.5 0.7 compare_select_fusion.2
  51.2 3.4 gather_fusion
  54.6 0.7 compare_and_fusion.1
  55.4 1.6 gather_fusion.1
  56.9 0.7 compare_select_fusion
  57.6 1.8 gather_fusion.2
  59.4 46.1 %all-gather.5.cloned.1.call-done = f32[128,8192]{1,0:T(8,128)} async-done(((f32[128,512]{1,0:T(8,128)}), f32[128,8192]{1,0:T(8,128)}) %all-gather.5.cloned.1.call-update) | async-done | bytes 4194320 | tf_op jit(solution)/shard_map/all_gather | solution.py:34
  105.5 13.0 %fusion = f32[128,256]{1,0:T(8,128)S(1)} fusion(f32[128,8192]{1,0:T(8,128)} %all-gather.5.cloned.1.call-done, f32[256,8192]{1,0:T(8,128)} %param.17), kind=kOutput, calls=%fused_computation.8 | convolution fusion | flops 3223322624 | bytes 12713984 | tf_op jit(solution)/shard_map/dot_general | solution.py:22
  118.5 65.2 %all-gather.3.cloned.1.call-done = f32[128,8192]{1,0:T(8,128)} async-done(((f32[128,512]{1,0:T(8,128)}), f32[128,8192]{1,0:T(8,128)}) %all-gather.3.cloned.1.call-update) | async-done | bytes 4194320 | tf_op jit(solution)/shard_map/all_gather | solution.py:33
  183.8 13.3 %select_select_fusion = (f32[128,256]{1,0:T(8,128)S(1)}, f32[128,256]{1,0:T(8,128)S(1)}) fusion(s32[128,256]{1,0:T(8,128)S(1)} %copy-done.3, f32[128,256]{1,0:T(8,128)S(1)} %fusion, f32[256]{0:T(256)S(1)} %copy-done.5, f32[128,8192]{1,0:T(8,128)} %all-gather.3.cloned.1.call-done, f32[256,8192]{1,0:T(8,128)} %param.17), kind=kOutput, calls=%fused_computation.23 | convolution fusion | flops 3221618688 | bytes 13108224 | tf_op jit(solution)/shard_map/dot_general | solution.py:21
  197.1 1.6 gather_fusion.3
  198.7 1.6 gather_fusion.6
  200.3 0.4 fusion.4
  200.7 18.5 %convolution_bitcast_fusion = f32[8192,512]{0,1:T(8,128)} fusion(f32[256,8192]{1,0:T(8,128)} %param.17, f32[512,256]{1,0:T(8,128)S(1)} %get-tuple-element.7, f32[512,256]{1,0:T(8,128)S(1)} %gather_fusion.3, pred[512]{0:T(512)(128)(4,1)S(1)} %get-tuple-element.10), kind=kOutput, calls=%fused_computation.7 | convolution fusion | flops 12885164032 | bytes 26214912 | tf_op jit(solution)/shard_map/dot_general | solution.py:45
  219.3 0.9 copy-done.2
  220.2 1.6 gather_fusion.4
  221.8 2.3 gather_fusion.5
  224.1 204.3 %reduce-scatter.2.cloned.1.call-done = f32[512,512]{0,1:T(8,128)} async-done(((f32[8192,512]{0,1:T(8,128)}), f32[512,512]{0,1:T(8,128)}) %reduce-scatter.2.cloned.1.call-update) | async-done | bytes 1048592 | tf_op jit(solution)/shard_map/reduce_scatter | solution.py:44
  428.4 2.0 fusion.3
  430.4 36.5 %psum.7 = f32[512]{0:T(512)} all-reduce(f32[512]{0:T(512)S(1)} %add_add_fusion), channel_id=1, replica_groups=mesh['spec'=16,'neuron'=16] {'neuron'}, use_global_device_ids=true, to_apply=%region_4.8 | all-reduce | flops 512 | bytes 4096 | tf_op jit(solution)/shard_map/psum | solution.py:53
  (20 shorter events, 0.2 us)
Async XLA Ops:
  7.2 48.2 %copy-start = (f32[1000,256]{1,0:T(8,128)S(1)}, f32[1000,256]{1,0:T(8,128)}, u32[]{:S(2)}) copy-start(f32[1000,256]{1,0:T(8,128)} %param.19) | copy-start | bytes 3072004
  7.2 52.2 %copy-start.4 = (s32[512]{0:T(512)S(1)}, s32[512]{0:T(512)}, u32[]{:S(2)}) copy-start(s32[512]{0:T(512)} %param.22) | copy-start | bytes 6148
  7.2 98.3 %all-gather.5.cloned.1.call-start = ((), (), s32[]{:S(2)}) async-start(), calls=%async_computation.2 | async-start | bytes 4456448 | tf_op jit(solution)/shard_map/all_gather | solution.py:34
  31.4 152.3 %all-gather.3.cloned.1.call-start = ((), (), s32[]{:S(2)}) async-start(), calls=%async_computation.1 | async-start | bytes 4456448 | tf_op jit(solution)/shard_map/all_gather | solution.py:33
  50.5 378.0 %reduce-scatter.2.cloned.1.call-start = ((), (), s32[]{:S(2)}) async-start(), calls=%async_computation.3 | async-start | bytes 17825792 | tf_op jit(solution)/shard_map/reduce_scatter | solution.py:44
  57.6 126.1 %copy-start.3 = (s32[128,256]{1,0:T(8,128)S(1)}, s32[128,256]{1,0:T(8,128)}, u32[]{:S(2)}) copy-start(s32[128,256]{1,0:T(8,128)} %param.20) | copy-start | bytes 393220
  57.6 126.1 %copy-start.5 = (f32[256]{0:T(256)S(1)}, f32[256]{0:T(256)}, u32[]{:S(2)}) copy-start(f32[256]{0:T(256)} %param.18) | copy-start | bytes 3076
  219.2 0.9 copy-start.2
  220.2 1.6 copy-start.1
Sparse Core Ops, SparseCore 0:
  31.6 73.9 all-gather.4
  108.0 75.7 all-gather.2
  219.4 208.9 reduce-scatter.1
where the time goes:
time: 480 us; the launch traced here: 473 us
  waiting for transfers between devices  316 us (66%)
  blocking collectives  79.6 us (17%)
  matrix products  44.9 us (9%)
  local copies, waits for them, and re-layouts  14.8 us (3%)
  between operations  13.9 us (3%)
    reduce_scatter x1, waiting for transfers between devices, local(): lax.psum_scatter(lax.dot_general(weight, scaled, (((0,), (1,)), ((), ()))...  204 us
    all_gather x1, waiting for transfers between devices, local(): lax.all_gather(center_all, 'neuron', axis=1, tiled=True)  65.2 us
    all_gather x1, waiting for transfers between devices, local(): lax.all_gather(radius_all, 'neuron', axis=1, tiled=True)  46.1 us
    psum x1, blocking collectives, local(): margin_bounds = lax.psum(input_part + relax_part, 'neuron')  36.5 us
    all_gather x1, blocking collectives, local(): lax.all_gather(radius, 'spec', axis=0, tiled=True)  24.2 us
    all_gather x1, blocking collectives, local(): lax.all_gather(center, 'spec', axis=0, tiled=True)  18.9 us
    dot_general x1, matrix products, local(): lax.dot_general(weight, scaled, (((0,), (1,)), ((), ())), precision=highest)  18.5 us
    dot_general x1, matrix products, interval(): lax.dot_general(center_full, weight, dims, precision=highest) + bias  13.3 us
  transfers between devices with their start and end apart: 3, of which 3 were waited for; matrix products, arithmetic and copies ran while one was open for 5% of the time, Pallas kernels for 0%

commit v1 on v0

v1 whole, which is shorter than its diff:
```python
import jax
import jax.numpy as jnp
from jax import lax
from jax.experimental import pallas as pl
from jax.experimental.pallas import tpu as pltpu
from jax.sharding import PartitionSpec as P

MESH = pl.DeviceIdType.MESH
F32, BF16 = jnp.float32, jnp.bfloat16


def split(v):
    hi = v.astype(BF16)
    return hi, (v - hi.astype(F32)).astype(BF16)


def dot(a, b):
    return lax.dot_general(a, b, (((1,), (0,)), ((), ())), preferred_element_type=F32)


def dot_t(a, b):
    return lax.dot_general(a, b, (((1,), (1,)), ((), ())), preferred_element_type=F32)


def sid(x, zl, c):
    return ((x + 4) % 4 * 2 + zl) * 2 + c


def nid(zh, y):
    return (zh + 4) % 4 * 4 + (y + 4) % 4


TILES = (
    (1, 0, 0, 0),
    (-1, 0, 0, 512),
    (0, 1, 0, 1024),
    (0, -1, 1, 1280),
    (1, 0, 1, 256),
    (-1, 0, 1, 768),
    (0, 0, 0, 1536),
    (0, 0, 1, 1792),
)
CLASS = ((0, 0), (2, 1), (0, 2), (2, 3))
N_SEM = 160


def kernel(
    center, radius, w, bias, ow, masks, labels, runner, simg, out, marg,
    wl, wb, owb, cb, ca, sa, sc, sh, sl, whi, wlo, sendb, recvb, crow, rrow, rel, eb, ob, mb, ss, rs, ls,
):
    s, n = lax.axis_index("spec"), lax.axis_index("neuron")
    x, zl, c = s // 4, s // 2 % 2, s % 2
    zh, y = n // 4, n % 4
    u = x * 2 + c

    started = []
    counter = [0]

    def take(k=1):
        counter[0] += k
        assert counter[0] <= N_SEM
        return counter[0] - k

    def send(src, dst, sem, dev):
        copy = pltpu.make_async_remote_copy(
            src_ref=src, dst_ref=dst, send_sem=ss.at[len(started)], recv_sem=rs.at[sem],
            device_id=dev, device_id_type=MESH,
        )
        copy.start()
        started.append(copy)

    def arrived(dst, sem):
        pltpu.make_async_copy(dst, dst, rs.at[sem]).wait()

    lc = [
        pltpu.make_async_copy(center, cb.at[y, zh, 0], ls.at[0]),
        pltpu.make_async_copy(radius, cb.at[y, zh, 1], ls.at[1]),
        pltpu.make_async_copy(ow, owb.at[0, 0:1000], ls.at[2]),
    ]
    for copy in lc:
        copy.start()
    wc = [
        pltpu.make_async_copy(w.at[:, pl.ds(i * 2048, 2048)], wl.at[:, pl.ds(i * 2048, 2048)], ls.at[3 + i])
        for i in range(4)
    ]
    for copy in wc:
        copy.start()

    peers = [(s, (n + d) % 16) for d in range(1, 16)]
    peers += [(sid(x + d, zl, c), n) for d in (1, 2, 3)]
    peers += [(sid(x, 1 - zl, c), n), (sid(x, zl, 1 - c), n)]
    peers += [(sid(x, 1 - zl, c), nid(zh + 2 * zl - 1, y + 2)), (sid(x, 1 - zl, c), nid(zh + 2, y))]
    barrier = pltpu.get_barrier_semaphore()
    for peer in peers:
        pl.semaphore_signal(barrier, inc=1, device_id=peer, device_id_type=MESH)
    pl.semaphore_wait(barrier, len(peers))

    lc[0].wait()
    lc[1].wait()
    cz, cy, cx = take(3), take(3), take(3)
    for d in (1, 2, 3):
        send(cb.at[y, zh], cb.at[y, zh], cz + d - 1, (s, nid(zh + d, y)))

    rows_o, rows_w = pl.ds(pl.multiple_of(120 * u, 8), 120), pl.ds(pl.multiple_of(32 * u, 32), 32)
    roles = [
        (sid(x, 0, c), zh + 2 * zl - 1, y + 2, 1 + 2 * zl),
        (sid(x, 1, c), zh + 2 * zl - 1, y + 2, 1 + 2 * zl),
        (sid(x, 1 - zl, c), zh + 2, y, 2),
    ]
    direct = {g: take(3) for g in "OAB"}
    for sd, zd, yd, j in roles:
        dev = (sd, nid(zd, yd))
        send(ow.at[rows_o], owb.at[j, rows_o], direct["O"] + j - 1, dev)
        send(ow.at[960:1000], owb.at[j, 960:1000], direct["O"] + j - 1, dev)
    for d in (1, 2, 3):
        send(cb.at[y, zh], ca.at[:, x, zl, c], cx + d - 1, (sid(x + d, zl, c), n))
    for sd, zd, yd, j in roles:
        dev = (sd, nid(zd, yd))
        for dy, dz, half, at in (TILES[0], TILES[1], TILES[2], TILES[3]):
            wide = 512 if dy else 256
            cols = pl.ds(pl.multiple_of(nid(zd + dz, yd + dy) * 512 + half * 256, 256), wide)
            send(w.at[rows_w, cols], wb.at[j - 1, rows_w, at : at + wide], direct["A"] + j - 1, dev)
    for sd, zd, yd, j in roles:
        dev = (sd, nid(zd, yd))
        cols = pl.ds(pl.multiple_of(nid(zd, yd) * 512, 512), 512)
        send(w.at[rows_w, cols], wb.at[j - 1, rows_w, 1536:2048], direct["B"] + j - 1, dev)

    def region(g, j, q, part=None):
        if g == "O":
            start, size = (0, 120) if part is None else ((0, 64), (64, 56))[part]
            return owb.at[j, pl.ds(pl.multiple_of(120 * q + start, 8), size)]
        start, size = (0, 32) if part is None else ((0, 16), (16, 16))[part]
        rows = pl.ds(pl.multiple_of(32 * q + start, 8), size)
        return wb.at[j - 1, rows, 0:1536] if g == "A" else wb.at[j - 1, rows, 1536:2048]

    left, right, sib = (sid(x - 1, zl, c), n), (sid(x + 1, zl, c), n), (sid(x, zl, 1 - c), n)
    ul, ur, uf = (x + 3) % 4 * 2 + c, (x + 1) % 4 * 2 + c, (x + 2) % 4 * 2 + c
    sem = {(g, j): take(5) for g in "OAB" for j in (1, 2, 3)}

    def pass_own(g, j):
        if g == "O":
            arrived(owb.at[j, 0:160], direct[g] + j - 1)
        else:
            arrived(region(g, j, u), direct[g] + j - 1)
        send(region(g, j, u), region(g, j, u), sem[g, j], right)
        send(region(g, j, u), region(g, j, u), sem[g, j] + 1, left)
        send(region(g, j, u), region(g, j, u), sem[g, j] + 4, sib)

    def pass_near(g, j):
        arrived(region(g, j, ul), sem[g, j])
        send(region(g, j, ul, 0), region(g, j, ul, 0), sem[g, j] + 2, right)
        send(region(g, j, ul), region(g, j, ul), sem[g, j] + 4, sib)
        arrived(region(g, j, ur), sem[g, j] + 1)
        send(region(g, j, ur, 1), region(g, j, ur, 1), sem[g, j] + 3, left)
        send(region(g, j, ur), region(g, j, ur), sem[g, j] + 4, sib)

    def pass_far(g, j):
        arrived(region(g, j, uf, 0), sem[g, j] + 2)
        arrived(region(g, j, uf, 1), sem[g, j] + 3)
        send(region(g, j, uf), region(g, j, uf), sem[g, j] + 4, sib)

    def whole(g, j):
        if g == "O":
            arrived(owb.at[j, 0:480], sem[g, j] + 4)
        elif g == "A":
            arrived(wb.at[j - 1, 0:128, 0:1536], sem[g, j] + 4)
        else:
            arrived(wb.at[j - 1, 0:128, 1536:2048], sem[g, j] + 4)

    for d in (1, 2, 3):
        arrived(cb.at[y, nid(zh - d, 0) // 4], cz + d - 1)
    for d in (1, 2, 3):
        send(cb.at[y], cb.at[y], cy + d - 1, (s, nid(zh, y + d)))

    img = jnp.transpose(jnp.broadcast_to(simg[...], (128, 512)))
    run = jnp.transpose(jnp.broadcast_to(runner[...], (128, 512)))[:, 0:1]
    picked = img == lax.broadcasted_iota(jnp.int32, (512, 128), 1)
    ob[...] = jnp.where(picked, 1.0, 0.0).astype(BF16)
    lab = jnp.sum(jnp.where(picked, labels[...].astype(F32), 0.0), axis=1, keepdims=True).astype(jnp.int32)
    for k in range(8):
        ids = lax.broadcasted_iota(jnp.int32, (512, 128), 1) + k * 128
        e = jnp.where(ids == lab, 1.0, 0.0) - jnp.where(ids == run, 1.0, 0.0)
        eb[:, k * 128 : (k + 1) * 128] = e.astype(BF16)
    for j in range(4):
        owb[j, 1000:1024, :] = jnp.zeros((24, 256), F32)

    for copy in wc:
        copy.wait()

    def pre_row(yy, carry):
        def body(k, carry):
            pc, pr = carry
            at = pl.multiple_of((k * 4 + yy) * 512, 512)
            chi, clo = split(cb[yy, k, 0])
            rhi, rlo = split(cb[yy, k, 1])
            cc, rr = jnp.concatenate([chi, clo], axis=0), jnp.concatenate([rhi, rlo], axis=0)
            wt = wl[:, pl.ds(at, 512)]
            thi, tlo = split(wt)
            pc = pc + dot_t(cc, thi) + dot_t(cc, tlo)
            thi, tlo = split(jnp.abs(wt))
            pr = pr + dot_t(rr, thi) + dot_t(rr, tlo)
            return pc, pr

        return lax.fori_loop(0, 4, body, carry)

    zero = jnp.zeros((16, 256), F32)
    carry = pre_row(y, (zero, zero))
    for j in (1, 2, 3):
        pass_own("O", j)
    for d in (1, 2, 3):
        arrived(cb.at[(y + 4 - d) % 4], cy + d - 1)
        carry = pre_row((y + 4 - d) % 4, carry)
    pc = carry[0][0:8] + carry[0][8:16] + bias[...]
    pr = carry[1][0:8] + carry[1][8:16]
    upper, lower = pc + pr, pc - pr
    slope = jnp.clip(upper / (upper - lower), 0.0, 1.0)
    m = masks[pl.ds(pl.multiple_of(8 * s, 8), 8), :]
    sa[0, x, zl, c] = jnp.where(m == 1, 1.0, jnp.where(m == 2, slope, 0.0))
    sa[4, x, zl, c] = jnp.where(m == 2, slope * lower, 0.0)
    sj = take(3)
    for j in (1, 2, 3):
        dy, dz = CLASS[j]
        send(sa.at[0, x, zl, c], sa.at[j, x, zl, c], sj + j - 1, (s, nid(zh - dz, y - dy)))

    for j in (1, 2, 3):
        pass_near("O", j)

    def gather_x(buf, base):
        for d in (1, 2, 3):
            arrived(buf.at[:, (x + 4 - d) % 4, zl, c], base + d - 1)

    cl, cc = take(), take()
    own = cb[y, zh]
    ca[:, x, zl, c] = own
    gather_x(ca, cx)
    send(ca.at[:, :, zl, c], ca.at[:, :, zl, c], cl, (sid(x, 1 - zl, c), n))

    for j in (1, 2, 3):
        arrived(sa.at[j, x, zl, c], sj + j - 1)
    sx, sz, sk = take(3), take(), take()
    for d in (1, 2, 3):
        send(sa.at[:, x, zl, c], sa.at[:, x, zl, c], sx + d - 1, (sid(x + d, zl, c), n))
    for j in (1, 2, 3):
        pass_far("O", j)
    for j in (1, 2, 3):
        pass_own("A", j)
    gather_x(sa, sx)
    send(sa.at[:, :, zl, c], sa.at[:, :, zl, c], sz, (sid(x, 1 - zl, c), n))
    arrived(ca.at[:, :, 1 - zl, c], cl)
    send(ca.at[:, :, :, c], ca.at[:, :, :, c], cc, sib)

    lc[2].wait()
    for j in (1, 2, 3):
        whole("O", j)

    def coeff(j, _):
        hi, lo = split(owb[j])
        e = eb[...]
        sc[j] = dot(e, hi) + dot(e, lo)
        return 0

    lax.fori_loop(0, 4, coeff, 0)

    for j in (1, 2, 3):
        pass_near("A", j)
    arrived(sa.at[:, :, 1 - zl, c], sz)
    send(sa.at[:, :, :, c], sa.at[:, :, :, c], sk, sib)
    for j in (1, 2, 3):
        pass_own("B", j)
    for j in (1, 2, 3):
        pass_far("A", j)
    arrived(sa.at[:, :, :, 1 - c], sk)

    def scale(j, _):
        hi, lo = split(sa[j].reshape(128, 256))
        o = ob[...]
        v = sc[j] * (dot(o, hi) + dot(o, lo))
        hi, lo = split(v)
        sh[j] = hi
        sl[j] = lo
        return 0

    lax.fori_loop(0, 4, scale, 0)
    hi, lo = split(sa[4].reshape(128, 256))
    off = dot(ob[...], hi) + dot(ob[...], lo)
    t = (sh[0].astype(F32) + sl[0].astype(F32)) * bias[...] - jnp.minimum(sc[0], 0.0) * off
    rel[...] = t[:, 0:128] + t[:, 128:256]

    for j in (1, 2, 3):
        whole("A", j)

    def tile(k):
        dy, dz, half, at = TILES[k]
        cols = pl.ds(pl.multiple_of(nid(zh + dz, y + dy) * 512 + half * 256, 256), 256)
        for j in range(4):
            hi, lo = split(wl[:, cols] if j == 0 else wb[j - 1, :, at : at + 256])
            whi[j * 256 : (j + 1) * 256, :] = hi
            wlo[j * 256 : (j + 1) * 256, :] = lo
        a = jnp.concatenate([sh[j] for j in range(4)], axis=1)
        b = jnp.concatenate([sl[j] for j in range(4)], axis=1)
        sendb[k] = dot(a, whi[...]) + dot(b, whi[...]) + dot(a, wlo[...])

    rt = take(6)
    for k in range(6):
        tile(k)
        dy, dz, _, _ = TILES[k]
        send(sendb.at[k], recvb.at[k], rt + k, (s, nid(zh + dz, y + dy)))
        if k < 3:
            pass_near("B", k + 1)
        else:
            pass_far("B", k - 2)

    arrived(ca.at[:, :, :, 1 - c], cc)
    for which, dst in ((0, crow), (1, rrow)):
        hi, lo = split(ca[which].reshape(128, 512))
        dst[...] = dot(ob[...], hi) + dot(ob[...], lo)
    for j in (1, 2, 3):
        whole("B", j)
    tile(6)
    tile(7)

    for half, ks in ((0, (0, 1, 2)), (1, (4, 5, 3))):
        cols = slice(half * 256, half * 256 + 256)
        v = sendb[6 + half]
        for k in ks:
            arrived(recvb.at[k], rt + k)
            v = v + recvb[k]
        out[:, cols] = v
        t = v * crow[:, cols] - jnp.abs(v) * rrow[:, cols]
        rel[...] += t[:, 0:128] + t[:, 128:256]

    mb[n] = jnp.sum(jnp.transpose(rel[...]), axis=0, keepdims=True)
    ms = take(15)
    for d in range(1, 16):
        send(mb.at[n], mb.at[n], ms + d - 1, (s, (n + d) % 16))
    for d in range(1, 16):
        arrived(mb.at[(n + 16 - d) % 16], ms + d - 1)
    marg[...] = jnp.sum(mb[...], axis=0)

    for copy in started:
        copy.wait_send()


def local(center, radius, weight, bias, out_weight, masks, image_labels, runner_up, spec_image):
    vmem, hbm = pl.BlockSpec(memory_space=pltpu.VMEM), pl.BlockSpec(memory_space=pl.ANY)
    coeffs, margins = pl.pallas_call(
        kernel,
        out_shape=(jax.ShapeDtypeStruct((512, 512), F32), jax.ShapeDtypeStruct((1, 512), F32)),
        in_specs=[hbm, hbm, hbm, vmem, hbm, vmem, vmem, vmem, vmem],
        out_specs=(vmem, vmem),
        scratch_shapes=[
            pltpu.VMEM((256, 8192), F32),
            pltpu.VMEM((3, 256, 2048), F32),
            pltpu.VMEM((4, 1024, 256), F32),
            pltpu.VMEM((4, 4, 2, 8, 512), F32),
            pltpu.VMEM((2, 4, 2, 2, 8, 512), F32),
            pltpu.VMEM((5, 4, 2, 2, 8, 256), F32),
            pltpu.VMEM((4, 512, 256), F32),
            pltpu.VMEM((4, 512, 256), BF16),
            pltpu.VMEM((4, 512, 256), BF16),
            pltpu.VMEM((1024, 256), BF16),
            pltpu.VMEM((1024, 256), BF16),
            pltpu.VMEM((8, 512, 256), F32),
            pltpu.VMEM((6, 512, 256), F32),
            pltpu.VMEM((512, 512), F32),
            pltpu.VMEM((512, 512), F32),
            pltpu.VMEM((512, 128), F32),
            pltpu.VMEM((512, 1024), BF16),
            pltpu.VMEM((512, 128), BF16),
            pltpu.VMEM((16, 1, 512), F32),
            pltpu.SemaphoreType.DMA((N_SEM,)),
            pltpu.SemaphoreType.DMA((N_SEM,)),
            pltpu.SemaphoreType.DMA((8,)),
        ],
        compiler_params=pltpu.CompilerParams(
            collective_id=0, has_side_effects=True, vmem_limit_bytes=60 * 1024 * 1024
        ),
        name="bounds",
    )(
        center,
        radius,
        weight,
        bias.reshape(1, 256),
        out_weight,
        masks,
        image_labels.reshape(1, 128),
        runner_up.reshape(1, 512),
        spec_image.reshape(1, 512),
    )
    return coeffs, margins.reshape(512)


def solution(mesh):
    return jax.shard_map(
        local,
        mesh=mesh,
        in_specs=(
            P("spec", "neuron"),
            P("spec", "neuron"),
            P("neuron", None),
            P("neuron"),
            P(None, "neuron"),
            P(None, "neuron"),
            P(),
            P("spec"),
            P("spec"),
        ),
        out_specs=(P("spec", "neuron"), P("spec")),
        check_vma=False,
    )
```

time: 480 us -> 128 us (0.27); the launches traced: 473 us -> 127 us
  waiting for transfers between devices: 316 us -> 0 us
  Pallas kernels: 0 us -> 123 us
  blocking collectives: 79.6 us -> 0 us
  matrix products: 44.9 us -> 0 us
  between operations: 13.9 us -> 0.64 us
  local copies, waits for them, and re-layouts: 14.8 us -> 3.52 us
    reduce_scatter x1 -> x0, waiting for transfers between devices: 204 us -> none  [local(): lax.psum_scatter(lax.dot_general(weight, scaled, (((0,), (1,)), ((), ()))...]
    pallas_call x0 -> x1, Pallas kernels: none -> 123 us  [local(): pl.pallas_call(kernel, out_shape=(jax.ShapeDtypeStruct((512, 512), F32),...]
    all_gather x2 -> x0, waiting for transfers between devices: 111 us -> none  [the longest x1 65.2 us: local(): lax.all_gather(center_all, 'neuron', axis=1, tiled=True)]
    dot_general x3 -> x0, matrix products: 44.9 us -> none  [the longest x1 18.5 us: local(): lax.dot_general(weight, scaled, (((0,), (1,)), ((), ())), precision=highest)]
    all_gather x2 -> x0, blocking collectives: 43.1 us -> none  [the longest x1 24.2 us: local(): lax.all_gather(radius, 'spec', axis=0, tiled=True)]
    psum x1 -> x0, blocking collectives: 36.5 us -> none  [local(): margin_bounds = lax.psum(input_part + relax_part, 'neuron')]
    gather x7 -> x0, local copies, waits for them, and re-layouts: 13.8 us -> none  [the longest x1 3.44 us: local(): true_class = jnp.take(image_labels, spec_image, axis=0)]
  transfers between devices with their start and end apart: 3 -> 0, of which waited for: 3 -> 0; matrix products, arithmetic and copies ran while one was open for 5% -> 0% of each run, Pallas kernels for 0% -> 0%
where the time goes in v1:
time: 128 us; the launch traced here: 127 us
  Pallas kernels  123 us (96%)
  local copies, waits for them, and re-layouts  3.52 us (3%)
    pallas_call x1, Pallas kernels, local(): pl.pallas_call(kernel, out_shape=(jax.ShapeDtypeStruct((512, 512), F32),...  123 us
    unnamed x2, local copies, waits for them, and re-layouts  3.52 us

profile of v1, /device:TPU:1, one launch (start us, length us, event | category | flops | bytes accessed | tf_op | source)
XLA Modules:
  0.0 127.1 jit_solution(1385255112674291202)
XLA Ops:
  0.6 122.9 %bounds.1 = (f32[512,512]{1,0:T(8,128)}, f32[1,512]{1,0:T(1,128)}) custom-call(f32[8,512]{1,0:T(8,128)} %center.1, f32[8,512]{1,0:T(8,128)} %radius.1, f32[256,8192]{1,0:T(8,128)} %w.1, f32[1,256]{1,0:T(1,128)} %bitcast.8, f32[1000,256]{1,0:T(8,128)} %ow.1, s32[128,256]{1,0:T(8,128)} %masks.1, s32[1,128]{1,0:T(1,128)} %bitcast.9, s32[1,512]{1,0:T(1,128)} %bitcast.6, ...), custom_call_target="tpu_custom_call" | custom-call | tf_op jit(solution)/shard_map/bounds/pallas_call | solution.py:346
  123.6 2.3 %copy.13 = f32[512,512]{1,0:T(8,128)} copy(f32[512,512]{1,0:T(8,128)} %get-tuple-element.8) | data formatting | bytes 2097152
  125.8 1.3 copy.14

commit v2 on v1

v2 whole, which is shorter than its diff:
```python
import jax
import jax.numpy as jnp
from jax import lax
from jax.experimental import pallas as pl
from jax.experimental.pallas import tpu as pltpu
from jax.sharding import PartitionSpec as P

MESH = pl.DeviceIdType.MESH
F32, BF16 = jnp.float32, jnp.bfloat16


def split(v):
    hi = v.astype(BF16)
    return hi, (v - hi.astype(F32)).astype(BF16)


def dot(a, b):
    return lax.dot_general(a, b, (((1,), (0,)), ((), ())), preferred_element_type=F32)


def dot_t(a, b):
    return lax.dot_general(a, b, (((1,), (1,)), ((), ())), preferred_element_type=F32)


def sid(x, zl, c):
    return ((x + 4) % 4 * 2 + zl) * 2 + c


def nid(zh, y):
    return (zh + 4) % 4 * 4 + (y + 4) % 4


TILES = ((1, 0, 0), (-1, 0, 0), (0, 1, 0), (0, -1, 1), (1, 0, 1), (-1, 0, 1), (0, 0, 0), (0, 0, 1))
SPAN = {"A": (0, 3), "B": (3, 6), "C": (6, 8)}
CLASS = ((0, 0), (2, 1), (0, 2), (2, 3))
N_SEND, N_RECV = 130, 130


def kernel(
    center, radius, w, bias, ow, masks, labels, runner, simg, out, marg,
    wl, wb, owb, cb, ca, sa, sc, sh, sl, whi, wlo, sendb, recvb, outb, crow, rrow, rel, eb, ob, mb, ss, rs, ls,
):
    s, n = lax.axis_index("spec"), lax.axis_index("neuron")
    x, zl, c = s // 4, s // 2 % 2, s % 2
    zh, y = n // 4, n % 4

    started = []
    counter = [0]

    def take(k=1):
        counter[0] += k
        assert counter[0] <= N_RECV
        return counter[0] - k

    def send(src, dst, sem, dev):
        copy = pltpu.make_async_remote_copy(
            src_ref=src, dst_ref=dst, send_sem=ss.at[len(started)], recv_sem=rs.at[sem],
            device_id=dev, device_id_type=MESH,
        )
        copy.start()
        started.append(copy)

    def arrived(dst, sem):
        pltpu.make_async_copy(dst, dst, rs.at[sem]).wait()

    lc = [
        pltpu.make_async_copy(center, cb.at[y, zh, 0], ls.at[0]),
        pltpu.make_async_copy(radius, cb.at[y, zh, 1], ls.at[1]),
        pltpu.make_async_copy(ow, owb.at[0, 0:1000], ls.at[2]),
    ]
    for copy in lc:
        copy.start()
    wc = [
        pltpu.make_async_copy(w.at[:, pl.ds(i * 2048, 2048)], wl.at[:, pl.ds(i * 2048, 2048)], ls.at[3 + i])
        for i in range(4)
    ]
    for copy in wc:
        copy.start()

    right, left, far = (sid(x + 1, zl, c), n), (sid(x - 1, zl, c), n), (sid(x + 2, zl, c), n)
    pair, sib = (sid(x, 1 - zl, c), n), (sid(x, zl, 1 - c), n)
    near = (sid(x, 1 - zl, c), nid(zh + 2 * zl - 1, y + 2))
    across = (sid(x, 1 - zl, c), nid(zh + 2, y))
    peers = [(s, (n + d) % 16) for d in range(1, 16)] + [right, left, far, pair, sib, near, across]
    barrier = pltpu.get_barrier_semaphore()
    for peer in peers:
        pl.semaphore_signal(barrier, inc=1, device_id=peer, device_id_type=MESH)
    pl.semaphore_wait(barrier, len(peers))

    lc[0].wait()
    lc[1].wait()
    cz, cy, cx = take(3), take(3), take(3)
    for d in (1, 2, 3):
        send(cb.at[y, zh], cb.at[y, zh], cz + d - 1, (s, nid(zh + d, y)))

    j_in, j_out = 3 - 2 * zl, 1 + 2 * zl
    order = (j_in, 2, j_out)
    groups = ("O", "A", "B", "C")
    base = {g: take(4 + 15) for g in groups}

    def part(g, j, q, which=None):
        if g == "O":
            start, size = ((0, 120), (0, 64), (64, 56))[0 if which is None else which + 1]
            return owb.at[j, pl.ds(pl.multiple_of(480 * c + 120 * q + start, 8), size)]
        start, size = ((0, 32), (0, 16), (16, 16))[0 if which is None else which + 1]
        lo, hi = SPAN[g]
        rows = pl.ds(pl.multiple_of(128 * c + 32 * q + start, 8), size)
        return wb.at[j - 1, rows, lo * 256 : hi * 256]

    def half_w(g, h):
        lo, hi = SPAN[g]
        return wb.at[1, pl.ds(pl.multiple_of(128 * c + 32 * x + 16 * h, 8), 16), lo * 256 : hi * 256]

    def half_o(h):
        start = 480 * c + 120 * x
        first = pl.ds(pl.multiple_of(start + 80 * h, 8), 40)
        second = pl.ds(pl.multiple_of(jnp.where(h == 0, start + 40, 960), 8), 40)
        return first, second

    def fetch(g):
        if g == "O":
            rows = pl.ds(pl.multiple_of(480 * c + 120 * x, 8), 120)
            send(ow.at[rows], owb.at[j_out, rows], base[g], near)
            send(ow.at[960:1000], owb.at[j_out, 960:1000], base[g], near)
            for rows in half_o(1 - zl):
                send(ow.at[rows], owb.at[2, rows], base[g] + 1, across)
            return
        lo, hi = SPAN[g]
        for dev, zd, yd, j, start, size in (
            (near, zh + 2 * zl - 1, y + 2, j_out, 0, 32),
            (across, zh + 2, y, 2, 16 * (1 - zl), 16),
        ):
            rows = pl.ds(pl.multiple_of(128 * c + 32 * x + start, 8), size)
            sem = base[g] + (0 if size == 32 else 1)
            k = lo
            while k < hi:
                dy, dz, half = TILES[k]
                wide = 512 if k == 6 else 256
                cols = pl.ds(pl.multiple_of(nid(zd + dz, yd + dy) * 512 + half * 256, 256), wide)
                send(w.at[rows, cols], wb.at[j - 1, rows, k * 256 : k * 256 + wide], sem, dev)
                k += wide // 256

    def ring(g, j):
        send(part(g, j, x), part(g, j, x), base[g] + 4 + 5 * (j - 1), right)
        send(part(g, j, x), part(g, j, x), base[g] + 5 + 5 * (j - 1), left)

    def pass_pair(g):
        if g == "O":
            arrived(owb.at[j_in, 0:160], base[g])
            send(part(g, j_in, x), part(g, j_in, x), base[g] + 2, pair)
            send(owb.at[j_in, 960:1000], owb.at[j_in, 960:1000], base[g] + 2, pair)
            arrived(owb.at[2, 0:80], base[g] + 1)
            for rows in half_o(zl):
                send(owb.at[2, rows], owb.at[2, rows], base[g] + 3, pair)
        else:
            arrived(part(g, j_in, x), base[g])
            send(part(g, j_in, x), part(g, j_in, x), base[g] + 2, pair)
            arrived(half_w(g, zl), base[g] + 1)
            send(half_w(g, zl), half_w(g, zl), base[g] + 3, pair)
        ring(g, j_in)

    def pass_own(g):
        if g == "O":
            arrived(owb.at[2, 0:80], base[g] + 3)
            ring(g, 2)
            arrived(owb.at[j_out, 0:160], base[g] + 2)
        else:
            arrived(half_w(g, 1 - zl), base[g] + 3)
            ring(g, 2)
            arrived(part(g, j_out, x), base[g] + 2)
        ring(g, j_out)

    xl, xr, xf = (x + 3) % 4, (x + 1) % 4, (x + 2) % 4

    def pass_near(g):
        for j in order:
            arrived(part(g, j, xl), base[g] + 4 + 5 * (j - 1))
            send(part(g, j, xl, 0), part(g, j, xl, 0), base[g] + 6 + 5 * (j - 1), right)
            arrived(part(g, j, xr), base[g] + 5 + 5 * (j - 1))
            send(part(g, j, xr, 1), part(g, j, xr, 1), base[g] + 7 + 5 * (j - 1), left)

    def core_half(g, j, cc):
        if g == "O":
            return owb.at[j, pl.ds(pl.multiple_of(480 * cc, 8), 480)]
        lo, hi = SPAN[g]
        return wb.at[j - 1, pl.ds(pl.multiple_of(128 * cc, 8), 128), lo * 256 : hi * 256]

    def pass_far(g):
        for j in order:
            arrived(part(g, j, xf, 0), base[g] + 6 + 5 * (j - 1))
            arrived(part(g, j, xf, 1), base[g] + 7 + 5 * (j - 1))
            send(core_half(g, j, c), core_half(g, j, c), base[g] + 8 + 5 * (j - 1), sib)

    def whole(g):
        for j in (1, 2, 3):
            arrived(core_half(g, j, 1 - c), base[g] + 8 + 5 * (j - 1))

    fetch("O")
    for d, dev in ((1, right), (2, far), (3, left)):
        send(cb.at[y, zh], ca.at[:, x, zl, c], cx + d - 1, dev)
    for d in (1, 2, 3):
        arrived(cb.at[y, (zh + 4 - d) % 4], cz + d - 1)
    for d in (1, 2, 3):
        send(cb.at[y], cb.at[y], cy + d - 1, (s, nid(zh, y + d)))
    fetch("A")

    img = jnp.transpose(jnp.broadcast_to(simg[...], (128, 512)))
    run = jnp.transpose(jnp.broadcast_to(runner[...], (128, 512)))[:, 0:1]
    picked = img == lax.broadcasted_iota(jnp.int32, (512, 128), 1)
    ob[...] = jnp.where(picked, 1.0, 0.0).astype(BF16)
    lab = jnp.sum(jnp.where(picked, labels[...].astype(F32), 0.0), axis=1, keepdims=True).astype(jnp.int32)
    for k in range(8):
        ids = lax.broadcasted_iota(jnp.int32, (512, 128), 1) + k * 128
        e = jnp.where(ids == lab, 1.0, 0.0) - jnp.where(ids == run, 1.0, 0.0)
        eb[:, k * 128 : (k + 1) * 128] = e.astype(BF16)
    for j in range(4):
        owb[j, 1000:1024, :] = jnp.zeros((24, 256), F32)
    ca[:, x, zl, c] = cb[y, zh]

    for copy in wc:
        copy.wait()

    def pre_row(yy, carry):
        def body(k, carry):
            pc, pr = carry
            at = pl.multiple_of((k * 4 + yy) * 512, 512)
            chi, clo = split(cb[yy, k, 0])
            rhi, rlo = split(cb[yy, k, 1])
            cc, rr = jnp.concatenate([chi, clo], axis=0), jnp.concatenate([rhi, rlo], axis=0)
            wt = wl[:, pl.ds(at, 512)]
            thi, tlo = split(wt)
            pc = pc + dot_t(cc, thi) + dot_t(cc, tlo)
            thi, tlo = split(jnp.abs(wt))
            pr = pr + dot_t(rr, thi) + dot_t(rr, tlo)
            return pc, pr

        return lax.fori_loop(0, 4, body, carry)

    pass_pair("O")
    zero = jnp.zeros((16, 256), F32)
    carry = pre_row(y, (zero, zero))
    pass_own("O")
    fetch("B")
    for d in (1, 2, 3):
        arrived(cb.at[(y + 4 - d) % 4], cy + d - 1)
        carry = pre_row((y + 4 - d) % 4, carry)
    pc = carry[0][0:8] + carry[0][8:16] + bias[...]
    pr = carry[1][0:8] + carry[1][8:16]
    upper, lower = pc + pr, pc - pr
    slope = jnp.clip(upper / (upper - lower), 0.0, 1.0)
    m = masks[pl.ds(pl.multiple_of(8 * s, 8), 8), :]
    sa[0, x, zl, c] = jnp.where(m == 1, 1.0, jnp.where(m == 2, slope, 0.0))
    sa[4, x, zl, c] = jnp.where(m == 2, slope * lower, 0.0)
    sj = take(3)
    for j in (1, 2, 3):
        dy, dz = CLASS[j]
        send(sa.at[0, x, zl, c], sa.at[j, x, zl, c], sj + j - 1, (s, nid(zh - dz, y - dy)))
    fetch("C")

    def gather_x(buf, sem):
        for d in (1, 2, 3):
            arrived(buf.at[:, (x + 4 - d) % 4, zl, c], sem + d - 1)

    pass_pair("A")
    pass_near("O")
    pass_own("A")
    cl, ck = take(), take()
    gather_x(ca, cx)
    send(ca.at[:, :, zl, c], ca.at[:, :, zl, c], cl, pair)
    for j in (1, 2, 3):
        arrived(sa.at[j, x, zl, c], sj + j - 1)
    sx, sz, sk = take(3), take(), take()
    for d, dev in ((1, right), (2, far), (3, left)):
        send(sa.at[:, x, zl, c], sa.at[:, x, zl, c], sx + d - 1, dev)
    pass_far("O")
    pass_pair("B")
    pass_near("A")
    gather_x(sa, sx)
    send(sa.at[:, :, zl, c], sa.at[:, :, zl, c], sz, pair)
    pass_own("B")
    lc[2].wait()
    whole("O")

    def coeff(j, _):
        hi, lo = split(owb[j])
        e = eb[...]
        sc[j] = dot(e, hi) + dot(e, lo)
        return 0

    lax.fori_loop(0, 4, coeff, 0)

    pass_far("A")
    arrived(sa.at[:, :, 1 - zl, c], sz)
    send(sa.at[:, :, :, c], sa.at[:, :, :, c], sk, sib)
    arrived(ca.at[:, :, 1 - zl, c], cl)
    send(ca.at[:, :, :, c], ca.at[:, :, :, c], ck, sib)
    pass_pair("C")
    pass_near("B")
    pass_own("C")
    arrived(sa.at[:, :, :, 1 - c], sk)

    def scale(j, _):
        hi, lo = split(sa[j].reshape(128, 256))
        o = ob[...]
        v = sc[j] * (dot(o, hi) + dot(o, lo))
        hi, lo = split(v)
        sh[j] = hi
        sl[j] = lo
        return 0

    lax.fori_loop(0, 4, scale, 0)
    hi, lo = split(sa[4].reshape(128, 256))
    off = dot(ob[...], hi) + dot(ob[...], lo)
    t = (sh[0].astype(F32) + sl[0].astype(F32)) * bias[...] - jnp.minimum(sc[0], 0.0) * off
    rel[...] = t[:, 0:128] + t[:, 128:256]

    rt = take(6)

    def tile(k):
        dy, dz, half = TILES[k]
        block = nid(zh + dz, y + dy)
        cols = pl.ds(pl.multiple_of(block * 512 + half * 256, 256), 256)
        for j in range(4):
            hi, lo = split(wl[:, cols] if j == 0 else wb[j - 1, :, k * 256 : k * 256 + 256])
            whi[j * 256 : (j + 1) * 256, :] = hi
            wlo[j * 256 : (j + 1) * 256, :] = lo
        a = jnp.concatenate([sh[j] for j in range(4)], axis=1)
        b = jnp.concatenate([sl[j] for j in range(4)], axis=1)
        sendb[k] = dot(a, whi[...]) + dot(b, whi[...]) + dot(a, wlo[...])
        if k < 6:
            send(sendb.at[k], recvb.at[k], rt + k, (s, block))

    whole("A")
    for k in range(0, 3):
        tile(k)
    pass_far("B")
    pass_near("C")
    arrived(ca.at[:, :, :, 1 - c], ck)
    for which, dst in ((0, crow), (1, rrow)):
        hi, lo = split(ca[which].reshape(128, 512))
        dst[...] = dot(ob[...], hi) + dot(ob[...], lo)
    pass_far("C")
    whole("B")
    for k in range(3, 6):
        tile(k)
    whole("C")
    tile(6)
    tile(7)

    written = []
    for half, ks in ((0, (0, 1, 2)), (1, (3, 4, 5))):
        cols = slice(half * 256, half * 256 + 256)
        v = sendb[6 + half]
        for k in ks:
            arrived(recvb.at[k], rt + k)
            v = v + recvb[k]
        outb[half] = v
        written.append(pltpu.make_async_copy(outb.at[half], out.at[:, cols], ls.at[half]))
        written[-1].start()
        t = v * crow[:, cols] - jnp.abs(v) * rrow[:, cols]
        rel[...] += t[:, 0:128] + t[:, 128:256]

    mb[n] = jnp.sum(jnp.transpose(rel[...]), axis=0, keepdims=True)
    ms = take(15)
    for d in range(1, 16):
        send(mb.at[n], mb.at[n], ms + d - 1, (s, (n + d) % 16))
    for d in range(1, 16):
        arrived(mb.at[(n + 16 - d) % 16], ms + d - 1)
    marg[...] = jnp.sum(mb[...], axis=0)

    for copy in written:
        copy.wait()
    for copy in started:
        copy.wait_send()


def local(center, radius, weight, bias, out_weight, masks, image_labels, runner_up, spec_image):
    vmem, hbm = pl.BlockSpec(memory_space=pltpu.VMEM), pl.BlockSpec(memory_space=pl.ANY)
    coeffs, margins = pl.pallas_call(
        kernel,
        out_shape=(jax.ShapeDtypeStruct((512, 512), F32), jax.ShapeDtypeStruct((1, 512), F32)),
        in_specs=[hbm, hbm, hbm, vmem, hbm, vmem, vmem, vmem, vmem],
        out_specs=(hbm, vmem),
        scratch_shapes=[
            pltpu.VMEM((256, 8192), F32),
            pltpu.VMEM((3, 256, 2048), F32),
            pltpu.VMEM((4, 1024, 256), F32),
            pltpu.VMEM((4, 4, 2, 8, 512), F32),
            pltpu.VMEM((2, 4, 2, 2, 8, 512), F32),
            pltpu.VMEM((5, 4, 2, 2, 8, 256), F32),
            pltpu.VMEM((4, 512, 256), F32),
            pltpu.VMEM((4, 512, 256), BF16),
            pltpu.VMEM((4, 512, 256), BF16),
            pltpu.VMEM((1024, 256), BF16),
            pltpu.VMEM((1024, 256), BF16),
            pltpu.VMEM((8, 512, 256), F32),
            pltpu.VMEM((6, 512, 256), F32),
            pltpu.VMEM((2, 512, 256), F32),
            pltpu.VMEM((512, 512), F32),
            pltpu.VMEM((512, 512), F32),
            pltpu.VMEM((512, 128), F32),
            pltpu.VMEM((512, 1024), BF16),
            pltpu.VMEM((512, 128), BF16),
            pltpu.VMEM((16, 1, 512), F32),
            pltpu.SemaphoreType.DMA((N_SEND,)),
            pltpu.SemaphoreType.DMA((N_RECV,)),
            pltpu.SemaphoreType.DMA((8,)),
        ],
        compiler_params=pltpu.CompilerParams(
            collective_id=0, has_side_effects=True, vmem_limit_bytes=60 * 1024 * 1024
        ),
        name="bounds",
    )(
        center,
        radius,
        weight,
        bias.reshape(1, 256),
        out_weight,
        masks,
        image_labels.reshape(1, 128),
        runner_up.reshape(1, 512),
        spec_image.reshape(1, 512),
    )
    return coeffs, margins.reshape(512)


def solution(mesh):
    return jax.shard_map(
        local,
        mesh=mesh,
        in_specs=(
            P("spec", "neuron"),
            P("spec", "neuron"),
            P("neuron", None),
            P("neuron"),
            P(None, "neuron"),
            P(None, "neuron"),
            P(),
            P("spec"),
            P("spec"),
        ),
        out_specs=(P("spec", "neuron"), P("spec")),
        check_vma=False,
    )
```

time: 128 us -> 109 us (0.85)
  Pallas kernels: 123 us -> 104 us
    pallas_call x1, Pallas kernels: 123 us -> 104 us  [local(): pl.pallas_call(kernel, out_shape=(jax.ShapeDtypeStruct((512, 512), F32),...]
where the time goes in v2:
time: 109 us; the launch traced here: 108 us
  Pallas kernels  104 us (95%)
  local copies, waits for them, and re-layouts  3.52 us (3%)
    pallas_call x1, Pallas kernels, local(): pl.pallas_call(kernel, out_shape=(jax.ShapeDtypeStruct((512, 512), F32),...  104 us
    unnamed x2, local copies, waits for them, and re-layouts  3.52 us

profile of v2, /device:TPU:1, one launch (start us, length us, event | category | flops | bytes accessed | tf_op | source)
XLA Modules:
  0.0 108.4 jit_solution(15406049658268570723)
XLA Ops:
  0.6 104.3 %bounds.1 = (f32[512,512]{1,0:T(8,128)}, f32[1,512]{1,0:T(1,128)}) custom-call(f32[8,512]{1,0:T(8,128)} %center.1, f32[8,512]{1,0:T(8,128)} %radius.1, f32[256,8192]{1,0:T(8,128)} %w.1, f32[1,256]{1,0:T(1,128)} %bitcast.8, f32[1000,256]{1,0:T(8,128)} %ow.1, s32[128,256]{1,0:T(8,128)} %masks.1, s32[1,128]{1,0:T(1,128)} %bitcast.9, s32[1,512]{1,0:T(1,128)} %bitcast.6, ...), custom_call_target="tpu_custom_call" | custom-call | tf_op jit(solution)/shard_map/bounds/pallas_call | solution.py:379
  104.9 2.3 %copy.13 = f32[512,512]{1,0:T(8,128)} copy(f32[512,512]{1,0:T(8,128)} %get-tuple-element.8) | data formatting | bytes 2097152
  107.2 1.3 %copy.14 = f32[512]{0:T(512)} copy(f32[512]{0:T(512)} %bitcast.5) | data formatting | bytes 4096

commit v3 on v2

v3 whole, which is shorter than its diff:
```python
import jax
import jax.numpy as jnp
from jax import lax
from jax.experimental import pallas as pl
from jax.experimental.pallas import tpu as pltpu
from jax.sharding import PartitionSpec as P

MESH = pl.DeviceIdType.MESH
F32, BF16 = jnp.float32, jnp.bfloat16


def split(v):
    hi = v.astype(BF16)
    return hi, (v - hi.astype(F32)).astype(BF16)


def dot(a, b):
    return lax.dot_general(a, b, (((1,), (0,)), ((), ())), preferred_element_type=F32)


def dot_t(a, b):
    return lax.dot_general(a, b, (((1,), (1,)), ((), ())), preferred_element_type=F32)


def sid(x, zl, c):
    return ((x + 4) % 4 * 2 + zl) * 2 + c


def nid(zh, y):
    return (zh + 4) % 4 * 4 + (y + 4) % 4


TILES = ((0, 1, 0), (0, -1, 1), (1, 0, 0), (-1, 0, 0), (1, 0, 1), (-1, 0, 1), (0, 0, 0), (0, 0, 1))
SLOT = (0, 3, 1, 2, 4, 5)
TWICE = "BC"
SPAN = {"A": (0, 2), "B": (2, 4), "C": (4, 6), "D": (6, 8)}
CLASS = ((0, 0), (2, 1), (0, 2), (2, 3))
N_RECV = 69


def kernel(
    center, radius, w, bias, ow, masks, labels, runner, simg, out, marg,
    wl, whl, ahl, wb, owb, cb, ca, sa, sc, sh, sl, whi, wlo, sendb, recvb, outb, crow, rrow, rel, eb, ob, mb,
    bias_v, mask_v, ids_v, ss, rs, ls,
):
    s, n = lax.axis_index("spec"), lax.axis_index("neuron")
    x, zl, c = s // 4, s // 2 % 2, s % 2
    zh, y = n // 4, n % 4

    counter = [0]
    kinds = {
        "o": owb.at[0:3, 0:1000],
        "w": wb,
        "b": cb.at[0:3, 0:2],
        "by": cb,
        "bk": cb.at[0:2],
        "j": sa.at[0:3, 0, 0, 0],
        "sx": sa.at[:, 0:3, 0, 0],
        "s": sa.at[:, 0:3],
        "r": recvb,
        "m": mb.at[0:15],
    }

    def take(k=1):
        counter[0] += k
        assert counter[0] <= N_RECV
        return counter[0] - k

    def send(src, dst, sem, dev, kind):
        pltpu.make_async_remote_copy(
            src_ref=src, dst_ref=dst, send_sem=ss.at[list(kinds).index(kind)], recv_sem=rs.at[sem],
            device_id=dev, device_id_type=MESH,
        ).start()

    def arrived(dst, sem):
        pltpu.make_async_copy(dst, dst, rs.at[sem]).wait()

    lc = [
        pltpu.make_async_copy(center, cb.at[y, zh, 0], ls.at[0]),
        pltpu.make_async_copy(radius, cb.at[y, zh, 1], ls.at[1]),
        pltpu.make_async_copy(ow, owb.at[0, 0:1000], ls.at[2]),
    ]
    for copy in lc:
        copy.start()
    wc = [
        pltpu.make_async_copy(w.at[:, pl.ds(i * 2048, 2048)], wl.at[:, pl.ds(i * 2048, 2048)], ls.at[3 + i])
        for i in range(4)
    ]
    for copy in wc:
        copy.start()
    small = [
        pltpu.make_async_copy(bias, bias_v, ls.at[7]),
        pltpu.make_async_copy(masks.at[pl.ds(pl.multiple_of(8 * s, 8), 8)], mask_v, ls.at[8]),
        pltpu.make_async_copy(labels, ids_v.at[0:1, 0:128], ls.at[9]),
        pltpu.make_async_copy(runner, ids_v.at[1:2], ls.at[10]),
        pltpu.make_async_copy(simg, ids_v.at[2:3], ls.at[11]),
    ]
    for copy in small:
        copy.start()

    right, left, far = (sid(x + 1, zl, c), n), (sid(x - 1, zl, c), n), (sid(x + 2, zl, c), n)
    pair, sib = (sid(x, 1 - zl, c), n), (sid(x, zl, 1 - c), n)
    near = (sid(x, 1 - zl, c), nid(zh + 2 * zl - 1, y + 2))
    across = (sid(x, 1 - zl, c), nid(zh + 2, y))
    peers = [(s, (n + d) % 16) for d in range(1, 16)] + [right, left, far, pair, sib, near, across]
    barrier = pltpu.get_barrier_semaphore()
    for peer in peers:
        pl.semaphore_signal(barrier, inc=1, device_id=peer, device_id_type=MESH)
    pl.semaphore_wait(barrier, len(peers))

    lc[0].wait()
    lc[1].wait()
    cz, cy, cx = take(), take(3), take()
    for d in (1, 2, 3):
        send(cb.at[y, zh], cb.at[y, zh], cz, (s, nid(zh + d, y)), "b")

    j_in, j_out = 3 - 2 * zl, 1 + 2 * zl
    order = (j_in, 2, j_out)
    base = {g: take(11) for g in "OABCD"}
    xl, xr, xf = (x + 3) % 4, (x + 1) % 4, (x + 2) % 4

    def part_o(j, q, start=0, size=120):
        return owb.at[j, pl.ds(pl.multiple_of(480 * c + 120 * q + start, 8), size)]

    def half_o(h):
        start = 480 * c + 120 * x
        first = pl.ds(pl.multiple_of(start + 80 * h, 8), 40)
        second = pl.ds(pl.multiple_of(jnp.where(h == 0, start + 40, 960), 8), 40)
        return first, second

    def fetch_o():
        rows = pl.ds(pl.multiple_of(480 * c + 120 * x, 8), 120)
        send(ow.at[rows], owb.at[j_out, rows], base["O"], near, "o")
        send(ow.at[960:1000], owb.at[j_out, 960:1000], base["O"], near, "o")
        for rows in half_o(1 - zl):
            send(ow.at[rows], owb.at[2, rows], base["O"] + 1, across, "o")

    def ring_o(j):
        send(part_o(j, x), part_o(j, x), base["O"] + 3 + j, right, "o")
        send(part_o(j, x), part_o(j, x), base["O"] + 3 + j, left, "o")

    def pair_o_block():
        arrived(owb.at[j_in, 0:160], base["O"])
        ring_o(j_in)
        send(part_o(j_in, x), part_o(j_in, x), base["O"] + 2, pair, "o")
        send(owb.at[j_in, 960:1000], owb.at[j_in, 960:1000], base["O"] + 2, pair, "o")

    def pair_o_half():
        arrived(owb.at[2, 0:80], base["O"] + 1)
        for rows in half_o(zl):
            send(owb.at[2, rows], owb.at[2, rows], base["O"] + 3, pair, "o")

    def own_o():
        arrived(owb.at[2, 0:80], base["O"] + 3)
        ring_o(2)
        arrived(owb.at[j_out, 0:160], base["O"] + 2)
        ring_o(j_out)

    def near_o(js):
        for j in js:
            arrived(owb.at[j, 0:240], base["O"] + 3 + j)
            send(part_o(j, xl, 0, 64), part_o(j, xl, 0, 64), base["O"] + 6 + j, right, "o")
            send(part_o(j, xr, 64, 56), part_o(j, xr, 64, 56), base["O"] + 6 + j, left, "o")

    def far_o():
        for j in order:
            arrived(part_o(j, xf), base["O"] + 6 + j)
            rows = pl.ds(pl.multiple_of(480 * c, 8), 480)
            send(owb.at[j, rows], owb.at[j, rows], base["O"] + 10, sib, "o")

    def rows_w(start, size):
        return pl.ds(pl.multiple_of(128 * c + start, 16), size)

    def cols_w(g):
        lo, hi = SPAN[g]
        return slice(lo * 256, hi * 256)

    def part_w(g, j, q, start=0, size=32):
        return wb.at[j - 1, rows_w(64 * (q % 2) + 32 * (q // 2) + start, size), cols_w(g)]

    def block_in(g, j):
        return wb.at[j - 1, rows_w(64 * (x % 2), 64), cols_w(g)] if g in TWICE else part_w(g, j, x)

    def half_in(g, h):
        if g in TWICE:
            return wb.at[1, rows_w(64 * (x % 2) + 32 * h, 32), cols_w(g)]
        return part_w(g, 2, x, 16 * h, 16)

    def fetch(g):
        lo, hi = SPAN[g]
        unit = 64 if g in TWICE else 32
        first = 64 * (x % 2) + (0 if g in TWICE else 32 * (x // 2))
        for dev, zd, yd, j, start, size in (
            (near, zh + 2 * zl - 1, y + 2, j_out, 0, unit),
            (across, zh + 2, y, 2, unit // 2 * (1 - zl), unit // 2),
        ):
            rows = rows_w(first + start, size)
            k = lo
            while k < hi:
                dy, dz, half = TILES[k]
                wide = 512 if k == 6 else 256
                cols = pl.ds(pl.multiple_of(nid(zd + dz, yd + dy) * 512 + half * 256, 256), wide)
                sem = base[g] + (0 if size == unit else 1)
                send(w.at[rows, cols], wb.at[j - 1, rows, k * 256 : k * 256 + wide], sem, dev, "w")
                k += wide // 256

    def pair_w(g):
        arrived(block_in(g, j_in), base[g])
        send(block_in(g, j_in), block_in(g, j_in), base[g] + 2, pair, "w")
        arrived(half_in(g, zl), base[g] + 1)
        send(half_in(g, zl), half_in(g, zl), base[g] + 3, pair, "w")

    def ring_w(g, js=order):
        for j in js:
            if j is order[1]:
                arrived(half_in(g, 1 - zl), base[g] + 3)
            elif j is order[2]:
                arrived(block_in(g, j), base[g] + 2)
            send(part_w(g, j, x), part_w(g, j, x), base[g] + 3 + j, right, "w")
            send(part_w(g, j, x), part_w(g, j, x), base[g] + 3 + j, left, "w")

    def core_w(g):
        for j in order:
            arrived(wb.at[j - 1, 0:64, cols_w(g)], base[g] + 3 + j)
            half = wb.at[j - 1, rows_w(0, 128), cols_w(g)]
            send(half, half, base[g] + 10, sib, "w")

    def near_w(g, js=order):
        for j in js:
            arrived(wb.at[j - 1, 0:64, cols_w(g)], base[g] + 3 + j)
            send(part_w(g, j, xl, 0, 16), part_w(g, j, xl, 0, 16), base[g] + 6 + j, right, "w")
            send(part_w(g, j, xr, 16, 16), part_w(g, j, xr, 16, 16), base[g] + 6 + j, left, "w")

    def far_w(g):
        for j in order:
            arrived(part_w(g, j, xf), base[g] + 6 + j)
            half = wb.at[j - 1, rows_w(0, 128), cols_w(g)]
            send(half, half, base[g] + 10, sib, "w")

    def whole_w(g):
        arrived(wb.at[:, 0:128, cols_w(g)], base[g] + 10)

    fetch_o()
    for dev in (right, far, left):
        send(cb.at[y, zh], ca.at[:, x, zl, c], cx, dev, "b")
    for i in range(4):
        wc[i].wait()

        def parts(k, _):
            cols = pl.ds(pl.multiple_of(k * 256, 256), 256)
            v = wl[:, cols]
            whl[0, :, cols], whl[1, :, cols] = split(v)
            ahl[0, :, cols], ahl[1, :, cols] = split(jnp.abs(v))
            return 0

        lax.fori_loop(8 * i, 8 * i + 8, parts, 0)
    arrived(cb.at[0, 0:3], cz)
    for d in (1, 2, 3):
        send(cb.at[y], cb.at[y], cy + d - 1, (s, nid(zh, y + d)), "by")

    for copy in small:
        copy.wait()
    img = jnp.transpose(jnp.broadcast_to(ids_v[2:3], (128, 512)))
    run = jnp.transpose(jnp.broadcast_to(ids_v[1:2], (128, 512)))[:, 0:1]
    picked = img == lax.broadcasted_iota(jnp.int32, (512, 128), 1)
    ob[...] = jnp.where(picked, 1.0, 0.0).astype(BF16)
    label = ids_v[0:1, 0:128].astype(F32)
    lab = jnp.sum(jnp.where(picked, label, 0.0), axis=1, keepdims=True).astype(jnp.int32)
    for k in range(8):
        ids = lax.broadcasted_iota(jnp.int32, (512, 128), 1) + k * 128
        e = jnp.where(ids == lab, 1.0, 0.0) - jnp.where(ids == run, 1.0, 0.0)
        eb[:, k * 128 : (k + 1) * 128] = e.astype(BF16)
    for j in range(4):
        owb[j, 1000:1024, :] = jnp.zeros((24, 256), F32)
    ca[:, x, zl, c] = cb[y, zh]

    def pre_row(yy, carry):
        def body(k, carry):
            pc, pr = carry
            cols = pl.ds(pl.multiple_of((k * 4 + yy) * 512, 512), 512)
            chi, clo = split(cb[yy, k, 0])
            rhi, rlo = split(cb[yy, k, 1])
            cc, rr = jnp.concatenate([chi, clo], axis=0), jnp.concatenate([rhi, rlo], axis=0)
            pc = pc + dot_t(cc, whl[0, :, cols]) + dot_t(cc, whl[1, :, cols])
            pr = pr + dot_t(rr, ahl[0, :, cols]) + dot_t(rr, ahl[1, :, cols])
            return pc, pr

        return lax.fori_loop(0, 4, body, carry, unroll=True)

    zero = jnp.zeros((16, 256), F32)
    carry = pre_row(y, (zero, zero))
    pair_o_block()
    fetch("A")
    pair_o_half()
    def more(d, carry):
        arrived(cb.at[(y + 4 - d) % 4], cy + d - 1)
        return pre_row((y + 4 - d) % 4, carry)

    carry = more(1, carry)
    pair_w("A")
    ring_w("A", order[:1])
    fetch("B")
    own_o()
    carry = more(2, carry)
    carry = more(3, carry)
    pc = carry[0][0:8] + carry[0][8:16] + bias_v[...]
    pr = carry[1][0:8] + carry[1][8:16]
    upper, lower = pc + pr, pc - pr
    slope = jnp.clip(upper / (upper - lower), 0.0, 1.0)
    m = mask_v[...]
    sa[0, x, zl, c] = jnp.where(m == 1, 1.0, jnp.where(m == 2, slope, 0.0))
    sa[4, x, zl, c] = jnp.where(m == 2, slope * lower, 0.0)
    sj = take()
    for j in (1, 2, 3):
        dy, dz = CLASS[j]
        send(sa.at[0, x, zl, c], sa.at[j, x, zl, c], sj, (s, nid(zh - dz, y - dy)), "j")
    fetch("C")
    near_o(order[:2])
    pair_w("B")
    near_o(order[2:])
    arrived(sa.at[0:3, 0, 0, 0], sj)
    sx, sz, sk = take(), take(), take()
    for dev in (right, far, left):
        send(sa.at[:, x, zl, c], sa.at[:, x, zl, c], sx, dev, "sx")
    ring_w("A", order[1:])
    ring_w("B", order[:1])
    far_o()
    arrived(sa.at[:, 0:3, 0, 0], sx)
    send(sa.at[:, :, zl, c], sa.at[:, :, zl, c], sz, pair, "s")
    fetch("D")
    near_w("A")
    pair_w("C")
    ring_w("B", order[1:])
    cl, ck = take(), take()
    arrived(ca.at[:, 0:3, 0, 0], cx)
    send(ca.at[:, :, zl, c], ca.at[:, :, zl, c], cl, pair, "by")
    lc[2].wait()
    arrived(owb.at[0:3, 0:480], base["O"] + 10)

    def coeff(k, _):
        e = eb[...]
        for j in (2 * k, 2 * k + 1):
            hi, lo = split(owb[j])
            sc[j] = dot(e, hi) + dot(e, lo)
        return 0

    lax.fori_loop(0, 2, coeff, 0)

    arrived(sa.at[:, :, 1 - zl, c], sz)
    send(sa.at[:, :, :, c], sa.at[:, :, :, c], sk, sib, "s")
    far_w("A")
    ring_w("C", order[:1])
    pair_w("D")
    arrived(sa.at[:, :, :, 1 - c], sk)

    def scale(k, _):
        o = ob[...]
        for j in (2 * k, 2 * k + 1):
            hi, lo = split(sa[j].reshape(128, 256))
            v = sc[j] * (dot(o, hi) + dot(o, lo))
            hi, lo = split(v)
            sh[j] = hi
            sl[j] = lo
        return 0

    lax.fori_loop(0, 2, scale, 0)
    rt = take(2)

    def prep(k):
        dy, dz, half = TILES[k]
        cols = pl.ds(pl.multiple_of(nid(zh + dz, y + dy) * 512 + half * 256, 256), 256)
        whi[k % 2, 0:256, :] = whl[0, :, cols]
        wlo[k % 2, 0:256, :] = whl[1, :, cols]
        for j in (1, 2, 3):
            hi, lo = split(wb[j - 1, :, k * 256 : k * 256 + 256])
            whi[k % 2, j * 256 : (j + 1) * 256, :] = hi
            wlo[k % 2, j * 256 : (j + 1) * 256, :] = lo

    def mul(k):
        a = jnp.concatenate([sh[j] for j in range(4)], axis=1)
        b = jnp.concatenate([sl[j] for j in range(4)], axis=1)
        for i in (0, 1):
            sendb[k + i] = dot(a, whi[i]) + dot(b, whi[i]) + dot(a, wlo[i])

    def pass_sum(k):
        dy, dz, half = TILES[k]
        send(sendb.at[k], recvb.at[SLOT[k]], rt + half, (s, nid(zh + dz, y + dy)), "r")

    whole_w("A")
    prep(0)
    prep(1)
    mul(0)
    pass_sum(0)
    pass_sum(1)
    core_w("B")
    ring_w("C", order[1:])
    whole_w("B")
    prep(2)
    prep(3)
    mul(2)
    pass_sum(2)
    pass_sum(3)
    ring_w("D")
    arrived(ca.at[:, :, 1 - zl, c], cl)
    send(ca.at[:, :, :, c], ca.at[:, :, :, c], ck, sib, "bk")
    core_w("C")
    whole_w("C")
    prep(4)
    prep(5)
    mul(4)
    pass_sum(4)
    pass_sum(5)
    hi, lo = split(sa[4].reshape(128, 256))
    off = dot(ob[...], hi) + dot(ob[...], lo)
    t = (sh[0].astype(F32) + sl[0].astype(F32)) * bias_v[...] - jnp.minimum(sc[0], 0.0) * off
    rel[...] = t[:, 0:128] + t[:, 128:256]
    near_w("D")
    arrived(ca.at[:, :, :, 1 - c], ck)
    for which, dst in ((0, crow), (1, rrow)):
        hi, lo = split(ca[which].reshape(128, 512))
        dst[...] = dot(ob[...], hi) + dot(ob[...], lo)
    far_w("D")
    whole_w("D")
    prep(6)
    prep(7)
    mul(6)

    written = []
    for half in (0, 1):
        cols = slice(half * 256, half * 256 + 256)
        arrived(recvb.at[0:3], rt + half)
        v = sendb[6 + half] + recvb[3 * half] + recvb[3 * half + 1] + recvb[3 * half + 2]
        outb[half] = v
        written.append(pltpu.make_async_copy(outb.at[half], out.at[:, cols], ls.at[half]))
        written[-1].start()
        t = v * crow[:, cols] - jnp.abs(v) * rrow[:, cols]
        rel[...] += t[:, 0:128] + t[:, 128:256]

    mb[n] = jnp.sum(jnp.transpose(rel[...]), axis=0, keepdims=True)
    ms = take()
    for d in range(1, 16):
        send(mb.at[n], mb.at[n], ms, (s, (n + d) % 16), "m")
    arrived(mb.at[0:15], ms)
    marg[...] = jnp.sum(mb[...], axis=0)

    for copy in written:
        copy.wait()
    for i, all_of_it in enumerate(kinds.values()):
        pltpu.make_async_copy(all_of_it, all_of_it, ss.at[i]).wait()


def finish(coeffs, margins, out, marg, held, row, sems):
    rows = [pl.ds(i * 128, 128) for i in range(4)]
    into = [pltpu.make_async_copy(coeffs.at[r], held.at[r], sems.at[i]) for i, r in enumerate(rows)]
    into.append(pltpu.make_async_copy(margins, row, sems.at[4]))
    back = [pltpu.make_async_copy(held.at[r], out.at[r], sems.at[5 + i]) for i, r in enumerate(rows)]
    back.append(pltpu.make_async_copy(row, marg, sems.at[9]))
    for copy in into:
        copy.start()
    for first, second in zip(into, back):
        first.wait()
        second.start()
    for copy in back:
        copy.wait()


def local(center, radius, weight, bias, out_weight, masks, image_labels, runner_up, spec_image):
    vmem, hbm = pl.BlockSpec(memory_space=pltpu.VMEM), pl.BlockSpec(memory_space=pl.ANY)
    coeffs, margins = pl.pallas_call(
        kernel,
        out_shape=(jax.ShapeDtypeStruct((512, 512), F32), jax.ShapeDtypeStruct((1, 512), F32)),
        in_specs=[hbm] * 9,
        out_specs=(hbm, vmem),
        scratch_shapes=[
            pltpu.VMEM((256, 8192), F32),
            pltpu.VMEM((2, 256, 8192), BF16),
            pltpu.VMEM((2, 256, 8192), BF16),
            pltpu.VMEM((3, 256, 2048), F32),
            pltpu.VMEM((4, 1024, 256), F32),
            pltpu.VMEM((4, 4, 2, 8, 512), F32),
            pltpu.VMEM((2, 4, 2, 2, 8, 512), F32),
            pltpu.VMEM((5, 4, 2, 2, 8, 256), F32),
            pltpu.VMEM((4, 512, 256), F32),
            pltpu.VMEM((4, 512, 256), BF16),
            pltpu.VMEM((4, 512, 256), BF16),
            pltpu.VMEM((2, 1024, 256), BF16),
            pltpu.VMEM((2, 1024, 256), BF16),
            pltpu.VMEM((8, 512, 256), F32),
            pltpu.VMEM((6, 512, 256), F32),
            pltpu.VMEM((2, 512, 256), F32),
            pltpu.VMEM((512, 512), F32),
            pltpu.VMEM((512, 512), F32),
            pltpu.VMEM((512, 128), F32),
            pltpu.VMEM((512, 1024), BF16),
            pltpu.VMEM((512, 128), BF16),
            pltpu.VMEM((16, 1, 512), F32),
            pltpu.VMEM((1, 256), F32),
            pltpu.VMEM((8, 256), jnp.int32),
            pltpu.VMEM((3, 512), jnp.int32),
            pltpu.SemaphoreType.DMA((10,)),
            pltpu.SemaphoreType.DMA((N_RECV,)),
            pltpu.SemaphoreType.DMA((12,)),
        ],
        compiler_params=pltpu.CompilerParams(
            collective_id=0, has_side_effects=True, vmem_limit_bytes=60 * 1024 * 1024
        ),
        name="bounds",
    )(
        center,
        radius,
        weight,
        bias.reshape(1, 256),
        out_weight,
        masks,
        image_labels.reshape(1, 128),
        runner_up.reshape(1, 512),
        spec_image.reshape(1, 512),
    )
    coeffs, margins = pl.pallas_call(
        finish,
        out_shape=(jax.ShapeDtypeStruct((512, 512), F32), jax.ShapeDtypeStruct((1, 512), F32)),
        in_specs=[hbm, hbm],
        out_specs=(hbm, hbm),
        scratch_shapes=[
            pltpu.VMEM((512, 512), F32),
            pltpu.VMEM((1, 512), F32),
            pltpu.SemaphoreType.DMA((10,)),
        ],
        name="finish",
    )(coeffs, margins)
    return coeffs, margins.reshape(512)


def solution(mesh):
    return jax.shard_map(
        local,
        mesh=mesh,
        in_specs=(
            P("spec", "neuron"),
            P("spec", "neuron"),
            P("neuron", None),
            P("neuron"),
            P(None, "neuron"),
            P(None, "neuron"),
            P(),
            P("spec"),
            P("spec"),
        ),
        out_specs=(P("spec", "neuron"), P("spec")),
        check_vma=False,
    )
```

time: 109 us -> 92.2 us (0.85)
  Pallas kernels: 104 us -> 91.3 us
  local copies, waits for them, and re-layouts: 3.52 us -> 0 us
    pallas_call x1, Pallas kernels: 104 us -> 89.3 us  [local(): pl.pallas_call(kernel, out_shape=(jax.ShapeDtypeStruct((512, 512), F32),...]
    unnamed x2 -> x0, local copies, waits for them, and re-layouts: 3.52 us -> none
    pallas_call x0 -> x1, Pallas kernels: none -> 2 us  [local(): pl.pallas_call(finish, out_shape=(jax.ShapeDtypeStruct((512, 512), F32),...]
where the time goes in v3:
time: 92.2 us; the launch traced here: 92.1 us
  Pallas kernels  91.3 us (99%)
    pallas_call x1, Pallas kernels, local(): pl.pallas_call(kernel, out_shape=(jax.ShapeDtypeStruct((512, 512), F32),...  89.3 us
    pallas_call x1, Pallas kernels, local(): pl.pallas_call(finish, out_shape=(jax.ShapeDtypeStruct((512, 512), F32),...  2 us

profile of v3, /device:TPU:1, one launch (start us, length us, event | category | flops | bytes accessed | tf_op | source)
XLA Modules:
  0.0 92.1 jit_solution(17072169953976266721)
XLA Ops:
  0.6 89.3 %bounds.1 = (f32[512,512]{1,0:T(8,128)}, f32[1,512]{1,0:T(1,128)}) custom-call(f32[8,512]{1,0:T(8,128)} %center.1, f32[8,512]{1,0:T(8,128)} %radius.1, f32[256,8192]{1,0:T(8,128)} %w.1, f32[1,256]{1,0:T(1,128)} %bitcast.7, f32[1000,256]{1,0:T(8,128)} %ow.1, s32[128,256]{1,0:T(8,128)} %masks.1, s32[1,128]{1,0:T(1,128)} %bitcast.8, s32[1,512]{1,0:T(1,128)} %bitcast.5, ...), custom_call_target="tpu_custom_call" | custom-call | tf_op jit(solution)/shard_map/bounds/pallas_call | solution.py:469
  90.0 2.0 %finish.1 = (f32[512,512]{1,0:T(8,128)}, f32[1,512]{1,0:T(1,128)}) custom-call(f32[512,512]{1,0:T(8,128)} %get-tuple-element.6.coeffs, f32[1,512]{1,0:T(1,128)} %get-tuple-element.7.margins), custom_call_target="tpu_custom_call" | custom-call | tf_op jit(solution)/shard_map/finish/pallas_call | solution.py:519

commit v4 on v3

--- a/solution.py
+++ b/solution.py
@@ -32,10 +32,10 @@
 
 TILES = ((0, 1, 0), (0, -1, 1), (1, 0, 0), (-1, 0, 0), (1, 0, 1), (-1, 0, 1), (0, 0, 0), (0, 0, 1))
 SLOT = (0, 3, 1, 2, 4, 5)
-TWICE = "BC"
+TWICE = "AB"
 SPAN = {"A": (0, 2), "B": (2, 4), "C": (4, 6), "D": (6, 8)}
 CLASS = ((0, 0), (2, 1), (0, 2), (2, 3))
-N_RECV = 69
+N_RECV = 73
 
 
 def kernel(
@@ -55,8 +55,8 @@
         "by": cb,
         "bk": cb.at[0:2],
         "j": sa.at[0:3, 0, 0, 0],
-        "sx": sa.at[:, 0:3, 0, 0],
-        "s": sa.at[:, 0:3],
+        "sx": owb.at[0, 0:280],
+        "s": sa.at[:, 0:2],
         "r": recvb,
         "m": mb.at[0:15],
     }
@@ -80,14 +80,6 @@
         pltpu.make_async_copy(radius, cb.at[y, zh, 1], ls.at[1]),
         pltpu.make_async_copy(ow, owb.at[0, 0:1000], ls.at[2]),
     ]
-    for copy in lc:
-        copy.start()
-    wc = [
-        pltpu.make_async_copy(w.at[:, pl.ds(i * 2048, 2048)], wl.at[:, pl.ds(i * 2048, 2048)], ls.at[3 + i])
-        for i in range(4)
-    ]
-    for copy in wc:
-        copy.start()
     small = [
         pltpu.make_async_copy(bias, bias_v, ls.at[7]),
         pltpu.make_async_copy(masks.at[pl.ds(pl.multiple_of(8 * s, 8), 8)], mask_v, ls.at[8]),
@@ -95,17 +87,38 @@
         pltpu.make_async_copy(runner, ids_v.at[1:2], ls.at[10]),
         pltpu.make_async_copy(simg, ids_v.at[2:3], ls.at[11]),
     ]
-    for copy in small:
+    wc = [
+        pltpu.make_async_copy(w.at[:, pl.ds(i * 2048, 2048)], wl.at[:, pl.ds(i * 2048, 2048)], ls.at[3 + i])
+        for i in range(4)
+    ]
+    for copy in lc[:2] + small:
         copy.start()
 
     right, left, far = (sid(x + 1, zl, c), n), (sid(x - 1, zl, c), n), (sid(x + 2, zl, c), n)
     pair, sib = (sid(x, 1 - zl, c), n), (sid(x, zl, 1 - c), n)
     near = (sid(x, 1 - zl, c), nid(zh + 2 * zl - 1, y + 2))
     across = (sid(x, 1 - zl, c), nid(zh + 2, y))
-    peers = [(s, (n + d) % 16) for d in range(1, 16)] + [right, left, far, pair, sib, near, across]
+    others = [(sid(x + d, zl + e - 2 * zl * e, c), n) for d in range(4) for e in (0, 1) if d or e]
+    peers = [(s, (n + d) % 16) for d in range(1, 16)] + others + [sib, near, across]
     barrier = pltpu.get_barrier_semaphore()
     for peer in peers:
         pl.semaphore_signal(barrier, inc=1, device_id=peer, device_id_type=MESH)
+    for copy in wc + lc[2:]:
+        copy.start()
+    for copy in small:
+        copy.wait()
+    img = jnp.transpose(jnp.broadcast_to(ids_v[2:3], (128, 512)))
+    run = jnp.transpose(jnp.broadcast_to(ids_v[1:2], (128, 512)))[:, 0:1]
+    picked = img == lax.broadcasted_iota(jnp.int32, (512, 128), 1)
+    ob[...] = jnp.where(picked, 1.0, 0.0).astype(BF16)
+    label = ids_v[0:1, 0:128].astype(F32)
+    lab = jnp.sum(jnp.where(picked, label, 0.0), axis=1, keepdims=True).astype(jnp.int32)
+    for k in range(8):
+        ids = lax.broadcasted_iota(jnp.int32, (512, 128), 1) + k * 128
+        e = jnp.where(ids == lab, 1.0, 0.0) - jnp.where(ids == run, 1.0, 0.0)
+        eb[:, k * 128 : (k + 1) * 128] = e.astype(BF16)
+    for j in range(4):
+        owb[j, 1000:1024, :] = jnp.zeros((24, 256), F32)
     pl.semaphore_wait(barrier, len(peers))
 
     lc[0].wait()
@@ -115,12 +128,16 @@
         send(cb.at[y, zh], cb.at[y, zh], cz, (s, nid(zh + d, y)), "b")
 
     j_in, j_out = 3 - 2 * zl, 1 + 2 * zl
-    order = (j_in, 2, j_out)
-    base = {g: take(11) for g in "OABCD"}
+    order = (j_in, j_out, 2)
+    base = {g: take(8 if g in TWICE else 11) for g in "OPABCD"}
     xl, xr, xf = (x + 3) % 4, (x + 1) % 4, (x + 2) % 4
 
-    def part_o(j, q, start=0, size=120):
-        return owb.at[j, pl.ds(pl.multiple_of(480 * c + 120 * q + start, 8), size)]
+    def part_o(g, j, q, start=0, size=120):
+        rows = pl.ds(pl.multiple_of(480 * c + 120 * q + start, 8), size)
+        return owb.at[j, rows, cols_o(g)]
+
+    def cols_o(g):
+        return slice(0, 128) if g == "O" else slice(128, 256)
 
     def half_o(h):
         start = 480 * c + 120 * x
@@ -128,45 +145,49 @@
         second = pl.ds(pl.multiple_of(jnp.where(h == 0, start + 40, 960), 8), 40)
         return first, second
 
-    def fetch_o():
-        rows = pl.ds(pl.multiple_of(480 * c + 120 * x, 8), 120)
-        send(ow.at[rows], owb.at[j_out, rows], base["O"], near, "o")
-        send(ow.at[960:1000], owb.at[j_out, 960:1000], base["O"], near, "o")
+    def fetch_o(g):
+        for rows in (pl.ds(pl.multiple_of(480 * c + 120 * x, 8), 120), slice(960, 1000)):
+            send(ow.at[rows, cols_o(g)], owb.at[j_out, rows, cols_o(g)], base[g], near, "o")
+
+    def fetch_o_half(g):
         for rows in half_o(1 - zl):
-            send(ow.at[rows], owb.at[2, rows], base["O"] + 1, across, "o")
-
-    def ring_o(j):
-        send(part_o(j, x), part_o(j, x), base["O"] + 3 + j, right, "o")
-        send(part_o(j, x), part_o(j, x), base["O"] + 3 + j, left, "o")
-
-    def pair_o_block():
-        arrived(owb.at[j_in, 0:160], base["O"])
-        ring_o(j_in)
-        send(part_o(j_in, x), part_o(j_in, x), base["O"] + 2, pair, "o")
-        send(owb.at[j_in, 960:1000], owb.at[j_in, 960:1000], base["O"] + 2, pair, "o")
-
-    def pair_o_half():
-        arrived(owb.at[2, 0:80], base["O"] + 1)
+            send(ow.at[rows, cols_o(g)], owb.at[2, rows, cols_o(g)], base[g] + 1, across, "o")
+
+    def ring_o(g, j):
+        send(part_o(g, j, x), part_o(g, j, x), base[g] + 3 + j, right, "o")
+        send(part_o(g, j, x), part_o(g, j, x), base[g] + 3 + j, left, "o")
+
+    def pair_o_block(g):
+        arrived(owb.at[j_in, 0:160, cols_o(g)], base[g])
+        ring_o(g, j_in)
+        send(part_o(g, j_in, x), part_o(g, j_in, x), base[g] + 2, pair, "o")
+        rest = owb.at[j_in, 960:1000, cols_o(g)]
+        send(rest, rest, base[g] + 2, pair, "o")
+
+    def pair_o_half(g):
+        arrived(owb.at[2, 0:80, cols_o(g)], base[g] + 1)
         for rows in half_o(zl):
-            send(owb.at[2, rows], owb.at[2, rows], base["O"] + 3, pair, "o")
-
-    def own_o():
-        arrived(owb.at[2, 0:80], base["O"] + 3)
-        ring_o(2)
-        arrived(owb.at[j_out, 0:160], base["O"] + 2)
-        ring_o(j_out)
-
-    def near_o(js):
+            send(owb.at[2, rows, cols_o(g)], owb.at[2, rows, cols_o(g)], base[g] + 3, pair, "o")
+
+    def own_o_out(g):
+        arrived(owb.at[j_out, 0:160, cols_o(g)], base[g] + 2)
+        ring_o(g, j_out)
+
+    def own_o_half(g):
+        arrived(owb.at[2, 0:80, cols_o(g)], base[g] + 3)
+        ring_o(g, 2)
+
+    def near_o(g, js=order):
         for j in js:
-            arrived(owb.at[j, 0:240], base["O"] + 3 + j)
-            send(part_o(j, xl, 0, 64), part_o(j, xl, 0, 64), base["O"] + 6 + j, right, "o")
-            send(part_o(j, xr, 64, 56), part_o(j, xr, 64, 56), base["O"] + 6 + j, left, "o")
-
-    def far_o():
+            arrived(owb.at[j, 0:240, cols_o(g)], base[g] + 3 + j)
+            send(part_o(g, j, xl, 0, 64), part_o(g, j, xl, 0, 64), base[g] + 6 + j, right, "o")
+            send(part_o(g, j, xr, 64, 56), part_o(g, j, xr, 64, 56), base[g] + 6 + j, left, "o")
+
+    def far_o(g):
         for j in order:
-            arrived(part_o(j, xf), base["O"] + 6 + j)
+            arrived(part_o(g, j, xf), base[g] + 6 + j)
             rows = pl.ds(pl.multiple_of(480 * c, 8), 480)
-            send(owb.at[j, rows], owb.at[j, rows], base["O"] + 10, sib, "o")
+            send(owb.at[j, rows, cols_o(g)], owb.at[j, rows, cols_o(g)], base[g] + 10, sib, "o")
 
     def rows_w(start, size):
         return pl.ds(pl.multiple_of(128 * c + start, 16), size)
@@ -213,9 +234,9 @@
     def ring_w(g, js=order):
         for j in js:
             if j is order[1]:
+                arrived(block_in(g, j), base[g] + 2)
+            elif j is order[2]:
                 arrived(half_in(g, 1 - zl), base[g] + 3)
-            elif j is order[2]:
-                arrived(block_in(g, j), base[g] + 2)
             send(part_w(g, j, x), part_w(g, j, x), base[g] + 3 + j, right, "w")
             send(part_w(g, j, x), part_w(g, j, x), base[g] + 3 + j, left, "w")
 
@@ -223,7 +244,7 @@
         for j in order:
             arrived(wb.at[j - 1, 0:64, cols_w(g)], base[g] + 3 + j)
             half = wb.at[j - 1, rows_w(0, 128), cols_w(g)]
-            send(half, half, base[g] + 10, sib, "w")
+            send(half, half, base[g] + 7, sib, "w")
 
     def near_w(g, js=order):
         for j in js:
@@ -238,11 +259,18 @@
             send(half, half, base[g] + 10, sib, "w")
 
     def whole_w(g):
-        arrived(wb.at[:, 0:128, cols_w(g)], base[g] + 10)
-
-    fetch_o()
+        arrived(wb.at[:, 0:128, cols_w(g)], base[g] + (7 if g in TWICE else 10))
+
+    for g in "OP":
+        fetch_o(g)
+    for g in "OP":
+        fetch_o_half(g)
     for dev in (right, far, left):
         send(cb.at[y, zh], ca.at[:, x, zl, c], cx, dev, "b")
+    arrived(cb.at[0, 0:3], cz)
+    for d in (1, 2, 3):
+        send(cb.at[y], cb.at[y], cy + d - 1, (s, nid(zh, y + d)), "by")
+
     for i in range(4):
         wc[i].wait()
 
@@ -254,24 +282,6 @@
             return 0
 
         lax.fori_loop(8 * i, 8 * i + 8, parts, 0)
-    arrived(cb.at[0, 0:3], cz)
-    for d in (1, 2, 3):
-        send(cb.at[y], cb.at[y], cy + d - 1, (s, nid(zh, y + d)), "by")
-
-    for copy in small:
-        copy.wait()
-    img = jnp.transpose(jnp.broadcast_to(ids_v[2:3], (128, 512)))
-    run = jnp.transpose(jnp.broadcast_to(ids_v[1:2], (128, 512)))[:, 0:1]
-    picked = img == lax.broadcasted_iota(jnp.int32, (512, 128), 1)
-    ob[...] = jnp.where(picked, 1.0, 0.0).astype(BF16)
-    label = ids_v[0:1, 0:128].astype(F32)
-    lab = jnp.sum(jnp.where(picked, label, 0.0), axis=1, keepdims=True).astype(jnp.int32)
-    for k in range(8):
-        ids = lax.broadcasted_iota(jnp.int32, (512, 128), 1) + k * 128
-        e = jnp.where(ids == lab, 1.0, 0.0) - jnp.where(ids == run, 1.0, 0.0)
-        eb[:, k * 128 : (k + 1) * 128] = e.astype(BF16)
-    for j in range(4):
-        owb[j, 1000:1024, :] = jnp.zeros((24, 256), F32)
     ca[:, x, zl, c] = cb[y, zh]
 
     def pre_row(yy, carry):
@@ -289,18 +299,23 @@
 
     zero = jnp.zeros((16, 256), F32)
     carry = pre_row(y, (zero, zero))
-    pair_o_block()
+    pair_o_block("O")
+    pair_o_block("P")
     fetch("A")
-    pair_o_half()
+    pair_o_half("O")
+    pair_o_half("P")
     def more(d, carry):
         arrived(cb.at[(y + 4 - d) % 4], cy + d - 1)
         return pre_row((y + 4 - d) % 4, carry)
 
     carry = more(1, carry)
+    own_o_out("O")
+    own_o_out("P")
     pair_w("A")
     ring_w("A", order[:1])
     fetch("B")
-    own_o()
+    own_o_half("O")
+    own_o_half("P")
     carry = more(2, carry)
     carry = more(3, carry)
     pc = carry[0][0:8] + carry[0][8:16] + bias_v[...]
@@ -314,28 +329,28 @@
     for j in (1, 2, 3):
         dy, dz = CLASS[j]
         send(sa.at[0, x, zl, c], sa.at[j, x, zl, c], sj, (s, nid(zh - dz, y - dy)), "j")
+    near_o("O", order[:2])
+    near_o("P", order[:2])
+    near_o("O", order[2:])
+    near_o("P", order[2:])
+    ring_w("A", order[1:])
+    pair_w("B")
     fetch("C")
-    near_o(order[:2])
-    pair_w("B")
-    near_o(order[2:])
+    fetch("D")
     arrived(sa.at[0:3, 0, 0, 0], sj)
-    sx, sz, sk = take(), take(), take()
-    for dev in (right, far, left):
+    sx, sk = take(), take()
+    for dev in others:
         send(sa.at[:, x, zl, c], sa.at[:, x, zl, c], sx, dev, "sx")
-    ring_w("A", order[1:])
-    ring_w("B", order[:1])
-    far_o()
-    arrived(sa.at[:, 0:3, 0, 0], sx)
-    send(sa.at[:, :, zl, c], sa.at[:, :, zl, c], sz, pair, "s")
-    fetch("D")
-    near_w("A")
-    pair_w("C")
-    ring_w("B", order[1:])
     cl, ck = take(), take()
     arrived(ca.at[:, 0:3, 0, 0], cx)
     send(ca.at[:, :, zl, c], ca.at[:, :, zl, c], cl, pair, "by")
+    far_o("O")
+    far_o("P")
+    ring_w("B", order[:1])
+    ring_w("B", order[1:])
     lc[2].wait()
-    arrived(owb.at[0:3, 0:480], base["O"] + 10)
+    for g in "OP":
+        arrived(owb.at[0:3, 0:480, cols_o(g)], base[g] + 10)
 
     def coeff(k, _):
         e = eb[...]
@@ -346,11 +361,13 @@
 
     lax.fori_loop(0, 2, coeff, 0)
 
-    arrived(sa.at[:, :, 1 - zl, c], sz)
+    arrived(owb.at[0, 0:280], sx)
     send(sa.at[:, :, :, c], sa.at[:, :, :, c], sk, sib, "s")
-    far_w("A")
+    core_w("A")
+    core_w("B")
+    pair_w("C")
+    pair_w("D")
     ring_w("C", order[:1])
-    pair_w("D")
     arrived(sa.at[:, :, :, 1 - c], sk)
 
     def scale(k, _):
@@ -392,7 +409,6 @@
     mul(0)
     pass_sum(0)
     pass_sum(1)
-    core_w("B")
     ring_w("C", order[1:])
     whole_w("B")
     prep(2)
@@ -400,10 +416,11 @@
     mul(2)
     pass_sum(2)
     pass_sum(3)
-    ring_w("D")
+    near_w("C")
     arrived(ca.at[:, :, 1 - zl, c], cl)
     send(ca.at[:, :, :, c], ca.at[:, :, :, c], ck, sib, "bk")
-    core_w("C")
+    ring_w("D")
+    far_w("C")
     whole_w("C")
     prep(4)
     prep(5)

time: 92.2 us -> 92.1 us (level)
  no operation moved by 1% of the time
where the time goes in v4:
time: 92.1 us; the launch traced here: 92 us
  Pallas kernels  91.2 us (99%)
    pallas_call x1, Pallas kernels, local(): pl.pallas_call(kernel, out_shape=(jax.ShapeDtypeStruct((512, 512), F32),...  89.2 us
    pallas_call x1, Pallas kernels, local(): pl.pallas_call(finish, out_shape=(jax.ShapeDtypeStruct((512, 512), F32),...  2 us

profile of v4, /device:TPU:1, one launch (start us, length us, event | category | flops | bytes accessed | tf_op | source)
XLA Modules:
  0.0 92.0 jit_solution(17389327286346264023)
XLA Ops:
  0.6 89.2 %bounds.1 = (f32[512,512]{1,0:T(8,128)}, f32[1,512]{1,0:T(1,128)}) custom-call(f32[8,512]{1,0:T(8,128)} %center.1, f32[8,512]{1,0:T(8,128)} %radius.1, f32[256,8192]{1,0:T(8,128)} %w.1, f32[1,256]{1,0:T(1,128)} %bitcast.7, f32[1000,256]{1,0:T(8,128)} %ow.1, s32[128,256]{1,0:T(8,128)} %masks.1, s32[1,128]{1,0:T(1,128)} %bitcast.8, s32[1,512]{1,0:T(1,128)} %bitcast.5, ...), custom_call_target="tpu_custom_call" | custom-call | tf_op jit(solution)/shard_map/bounds/pallas_call | solution.py:486
  89.8 2.0 %finish.1 = (f32[512,512]{1,0:T(8,128)}, f32[1,512]{1,0:T(1,128)}) custom-call(f32[512,512]{1,0:T(8,128)} %get-tuple-element.6.coeffs, f32[1,512]{1,0:T(1,128)} %get-tuple-element.7.margins), custom_call_target="tpu_custom_call" | custom-call | tf_op jit(solution)/shard_map/finish/pallas_call | solution.py:536

commit v5 on v4

--- a/solution.py
+++ b/solution.py
@@ -30,8 +30,8 @@
     return (zh + 4) % 4 * 4 + (y + 4) % 4
 
 
-TILES = ((0, 1, 0), (0, -1, 1), (1, 0, 0), (-1, 0, 0), (1, 0, 1), (-1, 0, 1), (0, 0, 0), (0, 0, 1))
-SLOT = (0, 3, 1, 2, 4, 5)
+TILES = ((1, 0, 0), (-1, 0, 0), (0, 1, 0), (0, -1, 1), (1, 0, 1), (-1, 0, 1), (0, 0, 0), (0, 0, 1))
+SLOT = (0, 1, 2, 3, 4, 5)
 TWICE = "AB"
 SPAN = {"A": (0, 2), "B": (2, 4), "C": (4, 6), "D": (6, 8)}
 CLASS = ((0, 0), (2, 1), (0, 2), (2, 3))

time: 92.1 us -> 88.9 us (0.965)
  Pallas kernels: 91.2 us -> 87.5 us
    pallas_call x1, Pallas kernels: 89.2 us -> 85.5 us  [local(): pl.pallas_call(kernel, out_shape=(jax.ShapeDtypeStruct((512, 512), F32),...]
where the time goes in v5:
time: 88.9 us; the launch traced here: 88.3 us
  Pallas kernels  87.5 us (98%)
    pallas_call x1, Pallas kernels, local(): pl.pallas_call(kernel, out_shape=(jax.ShapeDtypeStruct((512, 512), F32),...  85.5 us
    pallas_call x1, Pallas kernels, local(): pl.pallas_call(finish, out_shape=(jax.ShapeDtypeStruct((512, 512), F32),...  2 us

profile of v5, /device:TPU:1, one launch (start us, length us, event | category | flops | bytes accessed | tf_op | source)
XLA Modules:
  0.0 88.3 jit_solution(7401504622957594821)
XLA Ops:
  0.6 85.5 %bounds.1 = (f32[512,512]{1,0:T(8,128)}, f32[1,512]{1,0:T(1,128)}) custom-call(f32[8,512]{1,0:T(8,128)} %center.1, f32[8,512]{1,0:T(8,128)} %radius.1, f32[256,8192]{1,0:T(8,128)} %w.1, f32[1,256]{1,0:T(1,128)} %bitcast.7, f32[1000,256]{1,0:T(8,128)} %ow.1, s32[128,256]{1,0:T(8,128)} %masks.1, s32[1,128]{1,0:T(1,128)} %bitcast.8, s32[1,512]{1,0:T(1,128)} %bitcast.5, ...), custom_call_target="tpu_custom_call" | custom-call | tf_op jit(solution)/shard_map/bounds/pallas_call | solution.py:486
  86.1 2.0 %finish.1 = (f32[512,512]{1,0:T(8,128)}, f32[1,512]{1,0:T(1,128)}) custom-call(f32[512,512]{1,0:T(8,128)} %get-tuple-element.6.coeffs, f32[1,512]{1,0:T(1,128)} %get-tuple-element.7.margins), custom_call_target="tpu_custom_call" | custom-call | tf_op jit(solution)/shard_map/finish/pallas_call | solution.py:536

commit v6 on v5

--- a/solution.py
+++ b/solution.py
@@ -455,8 +455,8 @@
 
     mb[n] = jnp.sum(jnp.transpose(rel[...]), axis=0, keepdims=True)
     ms = take()
-    for d in range(1, 16):
-        send(mb.at[n], mb.at[n], ms, (s, (n + d) % 16), "m")
+    for dz, dy in [(dz, dy) for dz in (2, 1, 3, 0) for dy in (2, 1, 3, 0) if dz or dy]:
+        send(mb.at[n], mb.at[n], ms, (s, nid(zh + dz, y + dy)), "m")
     arrived(mb.at[0:15], ms)
     marg[...] = jnp.sum(mb[...], axis=0)
 

time: 88.9 us -> 88.8 us (level)
  no operation moved by 1% of the time
where the time goes in v6:
time: 88.8 us; the launch traced here: 88.4 us
  Pallas kernels  87.6 us (99%)
    pallas_call x1, Pallas kernels, local(): pl.pallas_call(kernel, out_shape=(jax.ShapeDtypeStruct((512, 512), F32),...  85.6 us
    pallas_call x1, Pallas kernels, local(): pl.pallas_call(finish, out_shape=(jax.ShapeDtypeStruct((512, 512), F32),...  2 us

profile of v6, /device:TPU:1, one launch (start us, length us, event | category | flops | bytes accessed | tf_op | source)
XLA Modules:
  0.0 88.4 jit_solution(17785929220842049327)
XLA Ops:
  0.6 85.6 %bounds.1 = (f32[512,512]{1,0:T(8,128)}, f32[1,512]{1,0:T(1,128)}) custom-call(f32[8,512]{1,0:T(8,128)} %center.1, f32[8,512]{1,0:T(8,128)} %radius.1, f32[256,8192]{1,0:T(8,128)} %w.1, f32[1,256]{1,0:T(1,128)} %bitcast.7, f32[1000,256]{1,0:T(8,128)} %ow.1, s32[128,256]{1,0:T(8,128)} %masks.1, s32[1,128]{1,0:T(1,128)} %bitcast.8, s32[1,512]{1,0:T(1,128)} %bitcast.5, ...), custom_call_target="tpu_custom_call" | custom-call | tf_op jit(solution)/shard_map/bounds/pallas_call | solution.py:486
  86.2 2.0 %finish.1 = (f32[512,512]{1,0:T(8,128)}, f32[1,512]{1,0:T(1,128)}) custom-call(f32[512,512]{1,0:T(8,128)} %get-tuple-element.6.coeffs, f32[1,512]{1,0:T(1,128)} %get-tuple-element.7.margins), custom_call_target="tpu_custom_call" | custom-call | tf_op jit(solution)/shard_map/finish/pallas_call | solution.py:536
